TPU v7x, 512 devices: a whole 4x8x8 slice. The times are simulated.
512 devices in a mesh: va: 32 (over x_lo, y, core), vb: 16 (over x_hi, z).
Axes of the slice: x: 4 (x_hi: 2, x_lo: 2; x = x_hi * 2 + x_lo), y: 8, z: 8, core: 2. Of those that a mesh axis runs over, the one named last changes fastest.
Arguments:
- amplitudes: bfloat16 [1024, 8, 65536], P('va', None, 'vb'), may hold values from -6 to 6
- integrals: bfloat16 [1024, 65536], P('va', 'vb'), may hold values from -0.125 to 0.125
- irrep_virt: int32 [1024], replicated, may hold values from 0 to 7
- irrep_occ: int32 [64], replicated, may hold values from 0 to 7, as said below
- irrep_slab: int32 [8], replicated, may hold values from 0 to 7
Outputs:
- cycle_term: bfloat16 [1024, 8192], P('vb', 'va')
Inputs may be any that keep to these rules, and one draw needn't show every extreme that they name: `irrep_virt`: D2h irrep labels. `irrep_occ`: D2h irrep labels; each aligned group of 8 consecutive orbitals k holds every label exactly once. `irrep_slab`: D2h irrep labels.
All inputs are finite; a program needn't handle non-finite values.
Results may differ from a plain program's by a relative error of at most 0.0015.
Values may be sent and summed in bfloat16 or wider, within the bound.
No kernel may reach another device: no remote copies, remote signals or barrier semaphores. Data moves between devices by JAX's collectives and lax.ppermute only.
A program may use at most 64 MiB of HBM per device.

v0:
```python
import jax
import jax.numpy as jnp
from jax import lax
from jax.sharding import PartitionSpec as P


def per_device(amplitudes, integrals, irrep_virt, irrep_occ, irrep_slab):
    a_rows, slab_count, pair_local = amplitudes.shape
    occ_count = irrep_occ.shape[0]
    c_local = pair_local // occ_count
    irr_first = lax.dynamic_slice_in_dim(irrep_virt, lax.axis_index("va") * a_rows, a_rows, 0)
    irr_second = lax.dynamic_slice_in_dim(irrep_virt, lax.axis_index("vb") * c_local, c_local, 0)
    pair_tag = jnp.bitwise_xor(irr_second[:, None], irrep_occ[None, :]).reshape(pair_local)
    left_tag = jnp.bitwise_xor(irr_first[:, None], irrep_slab[None, :])
    amp_sym = jnp.where(
        left_tag[:, :, None] == pair_tag[None, None, :], amplitudes, jnp.zeros_like(amplitudes)
    )
    flat_amp = amp_sym.reshape(a_rows * slab_count, pair_local)
    row_tag = jnp.bitwise_xor(irrep_virt, irrep_occ[0])
    gathered = lax.all_gather(integrals, "va", axis=0, tiled=True)
    int_sym = jnp.where(row_tag[:, None] == pair_tag[None, :], gathered, jnp.zeros_like(gathered))
    summed = lax.psum_scatter(
        lax.dot_general(
            int_sym, flat_amp, (((1,), (1,)), ((), ())), preferred_element_type=jnp.float32
        ),
        "vb",
        scatter_dimension=0,
        tiled=True,
    )
    return summed.astype(jnp.bfloat16)


def solution(mesh):
    placed = (P("va", None, "vb"), P("va", "vb"), P(), P(), P())
    return jax.shard_map(
        per_device, mesh=mesh, in_specs=placed, out_specs=P("vb", "va"), check_vma=False
    )
```

profile of v0, /device:TPU:8, one launch (start us, length us, event | category | flops | bytes accessed | tf_op | source)
XLA Modules:
  0.0 310.7 jit_solution(5064224351063463156)
XLA Ops:
  6.5 0.0 all-gather.2.cloned.1.call-start
  6.5 0.7 all-gather.2.cloned.1.call-update
  7.3 0.0 reduce-scatter.2.cloned.1.call-start
  7.3 0.8 dynamic_slice.7
  8.1 0.8 dynamic_slice.6
  8.8 0.7 broadcast_xor_fusion
  9.6 0.1 xor.52
  9.6 1.3 broadcast_xor_fusion.2
  11.0 0.7 broadcast_xor_fusion.1
  11.7 76.8 %all-gather.2.cloned.1.call-done = bf16[1024,4096]{1,0:T(8,128)(2,1)} async-done(((bf16[32,4096]{1,0:T(8,128)(2,1)}), bf16[1024,4096]{1,0:T(8,128)(2,1)}) %all-gather.2.cloned.1.call-update) | async-done | bytes 8388624 | tf_op jit(solution)/shard_map/all_gather | solution.py:20
  88.5 8.0 %fusion = f32[1024,256]{1,0:T(8,128)} fusion(bf16[1024,4096]{1,0:T(8,128)(2,1)} %all-gather.2.cloned.1.call-done, s32[4096]{0:T(1024)S(1)} %xor.52, s32[1024]{0:T(1024)S(1)} %broadcast_xor_fusion.2, bf16[32,8,4096]{2,1,0:T(8,128)(2,1)} %param.5, s32[32,8]{1,0:T(8,128)S(1)} %broadcast_xor_fusion.1), kind=kOutput, calls=%fused_computation.1 | convolution fusion | flops 2157969408 | bytes 11555840 | tf_op jit(solution)/shard_map/dot_general | solution.py:23
  96.5 0.0 reduce-scatter.2.cloned.1.call-update
  96.6 205.8 %reduce-scatter.2.cloned.1.call-done = f32[64,256]{1,0:T(8,128)} async-done(((f32[1024,256]{1,0:T(8,128)}), f32[64,256]{1,0:T(8,128)}) %reduce-scatter.2.cloned.1.call-update) | async-done | bytes 65552 | tf_op jit(solution)/shard_map/reduce_scatter | solution.py:22
  302.4 1.5 convert_element_type.3
Async XLA Ops:
  6.5 82.0 %all-gather.2.cloned.1.call-start = ((), (), s32[]{:S(2)}) async-start(), calls=%async_computation.1 | async-start | bytes 8650752 | tf_op jit(solution)/shard_map/all_gather | solution.py:20
  7.3 295.1 %reduce-scatter.2.cloned.1.call-start = ((), (), s32[]{:S(2)}) async-start(), calls=%async_computation.2 | async-start | bytes 1114112 | tf_op jit(solution)/shard_map/reduce_scatter | solution.py:22
Sparse Core Ops, SparseCore 0:
  9.5 78.9 all-gather.1
  96.7 205.6 reduce-scatter.1
where the time goes:
time: 311 us
  waiting for transfers between devices  283 us (91%)
  between operations  13.4 us (4%)
  matrix products  7.99 us (3%)
  other arithmetic  4.25 us (1%)
    reduce_scatter x1, waiting for transfers between devices, per_device(): lax.psum_scatter(lax.dot_general(int_sym, flat_amp, (((1,), (1,)), ((), (...  206 us
    all_gather x1, waiting for transfers between devices, per_device(): gathered = lax.all_gather(integrals, 'va', axis=0, tiled=True)  76.8 us
    dot_general x1, matrix products, per_device(): lax.dot_general(int_sym, flat_amp, (((1,), (1,)), ((), ())), preferred_el...  7.99 us
  transfers between devices with their start and end apart: 2, of which 2 were waited for; matrix products, arithmetic and copies ran while one was open for 1% of the time, Pallas kernels for 0%

commit v1 on v0

v1 whole, which is shorter than its diff:
```python
import functools

import jax
import jax.numpy as jnp
from jax import lax
from jax.experimental import pallas as pl
from jax.experimental.pallas import tpu as pltpu
from jax.sharding import Mesh, PartitionSpec as P

GROUP = 8
LANES = 128
WINDOW = 64
SLOTS = 24
BIG = 100 << 20

F32, BF16, I32 = jnp.float32, jnp.bfloat16, jnp.int32
SMEM = pl.BlockSpec(memory_space=pltpu.SMEM)
VMEM = pl.BlockSpec(memory_space=pltpu.VMEM)


def params(**more):
    return pltpu.CompilerParams(vmem_limit_bytes=48 << 20, **more)


def lanes(shape):
    return lax.broadcasted_iota(I32, shape, len(shape) - 1)


def rows_of(shape):
    return lax.broadcasted_iota(I32, shape, len(shape) - 2)


def spread(ref, start, count, position):
    out = jnp.zeros_like(position)
    for n in range(count):
        out = jnp.where(position == n, ref[start + n], out)
    return out


def occ_lanes(occ_ref):
    occ_count = occ_ref.shape[0]
    return spread(occ_ref, 0, occ_count, lanes((1, LANES)) % occ_count)


def pair_tags(occ, virt_ref, first_c, block, occ_count):
    per = LANES // occ_count
    c_of = lanes((1, LANES)) // occ_count
    return occ ^ spread(virt_ref, first_c + block * per, per, c_of)


def squeezer(width):
    shape = (width, width // GROUP)
    return jnp.where(rows_of(shape) // GROUP == lanes(shape), 1.0, 0.0).astype(BF16)


def first_of(axis_sizes):
    at = 0
    for name, size in axis_sizes:
        at = at * size + lax.axis_index(name)
    return at


def squeeze_int_kernel(va_axes, vb_axes, virt_ref, occ_ref, int_ref, out_ref):
    row_count, width = int_ref.shape
    occ_count = occ_ref.shape[0]
    c_count = width // occ_count
    va, vb = first_of(va_axes), first_of(vb_axes)
    occ = occ_lanes(occ_ref)
    row_tag = spread(virt_ref, va * row_count, row_count, rows_of((row_count, LANES))) ^ occ_ref[0]
    step = GROUP * LANES
    squeeze = squeezer(step)
    for part in range(width // step):
        kept = []
        for block in range(GROUP):
            at = part * GROUP + block
            tag = pair_tags(occ, virt_ref, vb * c_count, at, occ_count)
            held = int_ref[:, at * LANES : (at + 1) * LANES].astype(F32)
            kept.append(jnp.where(row_tag == tag, held, 0.0).astype(BF16))
        small = jnp.dot(jnp.concatenate(kept, 1), squeeze, preferred_element_type=F32).astype(BF16)
        for peer in range(out_ref.shape[0]):
            out_ref[peer, :, part * LANES : (part + 1) * LANES] = small


def squeeze_amp_kernel(va_axes, vb_axes, virt_ref, occ_ref, slab_ref, labels_ref, amp_ref, out_ref, most_ref):
    a_count, slab_count, width = amp_ref.shape
    occ_count = occ_ref.shape[0]
    part = pl.program_id(0)
    c_count = width // occ_count * pl.num_programs(0)
    va, vb = first_of(va_axes), first_of(vb_axes)
    occ = occ_lanes(occ_ref)
    slab = spread(slab_ref, 0, slab_count, rows_of((slab_count, LANES)))
    left = jnp.stack([slab ^ virt_ref[va * a_count + a] for a in range(a_count)])
    kept = []
    for block in range(GROUP):
        tag = pair_tags(occ, virt_ref, vb * c_count, part * GROUP + block, occ_count)
        held = amp_ref[:, :, block * LANES : (block + 1) * LANES].astype(F32)
        kept.append(jnp.where(left == tag[None], held, 0.0).reshape(a_count * slab_count, LANES).astype(BF16))
    out_ref[...] = jnp.dot(jnp.concatenate(kept, 1), squeezer(width), preferred_element_type=F32).astype(BF16)

    @pl.when(part == 0)
    def _():
        labels = labels_ref[...]
        half = lanes(labels.shape) // WINDOW
        most = jnp.int32(0)
        for label in range(GROUP):
            for side in range(LANES // WINDOW):
                hits = jnp.where((labels == label) & (half == side), 1, 0)
                most = jnp.maximum(most, jnp.max(jnp.sum(hits, axis=1, keepdims=True)))
        most_ref[0] = most


def sort_keys(labels):
    at = lanes(labels.shape)
    return (at // WINDOW) * (WINDOW * GROUP) + labels * WINDOW + at % WINDOW


def column_tags(va_axes, virt_ref, slab_ref, occ_ref, a_count):
    slab_count = slab_ref.shape[0]
    at = lanes((1, a_count * slab_count))
    first = spread(virt_ref, first_of(va_axes) * a_count, a_count, at // slab_count)
    return first ^ spread(slab_ref, 0, slab_count, at % slab_count) ^ occ_ref[0]


def multiply_kernel(slots, va_axes, virt_ref, occ_ref, slab_ref, labels_ref, own_ref, other_ref, amp_ref, out_ref, sorted_ref, tag_ref):
    windows, half_rows, depth = own_ref.shape
    core = lax.axis_index("c")
    columns = column_tags(va_axes, virt_ref, slab_ref, occ_ref, amp_ref.shape[0] // slab_ref.shape[0])
    labels = labels_ref[...]
    keys = sort_keys(labels)
    keys_down = jnp.transpose(keys.astype(F32))
    swap = (lanes(keys.shape) // half_rows) % 2 == 0
    def own_first(x):
        x = x.astype(F32)
        swapped = jnp.where(swap, pltpu.roll(x, LANES - half_rows, 1), pltpu.roll(x, half_rows, 1))
        return jnp.where(core == 0, x, swapped)
    keys_across, labels_across = own_first(keys), own_first(labels)
    square = (LANES, LANES)
    per = LANES // WINDOW
    for r in range(windows // per):
        before = jnp.where(keys_down[:, r : r + 1] < keys_across[r : r + 1, :], 1.0, 0.0)
        place = jnp.sum(before, axis=0, keepdims=True)
        moved = jnp.where(rows_of(square).astype(F32) == place, 1.0, 0.0)
        block = jnp.concatenate([x for w in range(r * per, (r + 1) * per) for x in (own_ref[w], other_ref[w])], 0)
        span = slice(r * LANES, (r + 1) * LANES)
        sorted_ref[span, :] = jnp.dot(moved.astype(BF16), block, preferred_element_type=F32).astype(BF16)
        tag_ref[span, :] = jnp.broadcast_to(
            jnp.sum(moved * labels_across[r : r + 1, :], axis=1, keepdims=True), square
        ).astype(I32)
    for r in range(windows // per):
        span = slice(r * LANES, (r + 1) * LANES)
        sums = lax.dot_general(
            sorted_ref[span, :], amp_ref[...], (((1,), (1,)), ((), ())), preferred_element_type=F32
        )
        tags = jnp.concatenate([tag_ref[span, :]] * (amp_ref.shape[0] // LANES), 1)
        sums = jnp.where(tags == columns, sums, 0.0)
        for w in range(per):
            part = sums[w * WINDOW : (w + 1) * WINDOW]
            total = part[:slots]
            for low in range(slots, WINDOW, slots):
                more = part[low : low + slots]
                if more.shape[0] < slots:
                    more = jnp.concatenate([more, jnp.zeros((slots - more.shape[0], more.shape[1]), F32)], 0)
                total = total + more
            out_ref[r * per + w] = total


def finish_kernel(slots, va_axes, vb_axes, virt_ref, occ_ref, slab_ref, labels_ref, parts_ref, out_ref):
    columns = column_tags(va_axes, virt_ref, slab_ref, occ_ref, out_ref.shape[1] // slab_ref.shape[0])
    vb = first_of(vb_axes)
    per = LANES // WINDOW
    total = parts_ref[0]
    for part in range(1, parts_ref.shape[0]):
        total = total + parts_ref[part]
    total = total.astype(BF16)
    row = labels_ref[pl.ds(vb // per, 1), :]
    mine = lanes(row.shape) // WINDOW == vb % per
    key = jnp.where(mine, row * WINDOW + lanes(row.shape) % WINDOW, WINDOW * GROUP).astype(F32)
    own = jnp.where(mine, lanes(row.shape) % WINDOW, -1)
    shape = (WINDOW, LANES)
    on_own = rows_of(shape) == own
    key_down = jnp.sum(jnp.where(on_own, key, 0.0), axis=1, keepdims=True)
    label_down = jnp.sum(jnp.where(on_own, row.astype(F32), 0.0), axis=1, keepdims=True).astype(I32)
    place = jnp.sum(jnp.where(key < key_down, 1.0, 0.0), axis=1, keepdims=True).astype(I32)
    pick = (WINDOW, slots)
    slot = jnp.where(place >= 2 * slots, place - 2 * slots, jnp.where(place >= slots, place - slots, place))
    chosen = jnp.where(lanes(pick) == slot, 1.0, 0.0).astype(BF16)
    full = jnp.dot(chosen, total, preferred_element_type=F32)
    out_ref[...] = jnp.where(label_down == columns, full, 0.0).astype(BF16)


def per_device(sizes, amplitudes, integrals, irrep_virt, irrep_occ, irrep_slab):
    va_axes = [(name, sizes[name]) for name in ("xl", "y", "c")]
    vb_axes = [(name, sizes[name]) for name in ("xh", "z")]
    a_rows, slab_count, width = amplitudes.shape
    b_rows = integrals.shape[0]
    depth = width // GROUP
    chips = sizes["xl"] * sizes["y"]
    labels = irrep_virt.reshape(-1, LANES)
    columns = a_rows * slab_count

    small = pl.pallas_call(
        functools.partial(squeeze_int_kernel, va_axes, vb_axes),
        out_shape=jax.ShapeDtypeStruct((chips, b_rows, depth), BF16),
        in_specs=[SMEM, SMEM, VMEM],
        out_specs=VMEM,
        compiler_params=params(),
        name="squeeze_int",
    )(irrep_virt, irrep_occ, integrals)
    own = lax.all_to_all(small, ("xl", "y"), 0, 0, tiled=False)
    other = lax.ppermute(own, "c", [(0, 1), (1, 0)])

    step = GROUP * LANES
    amp_small, most = pl.pallas_call(
        functools.partial(squeeze_amp_kernel, va_axes, vb_axes),
        grid=(width // step,),
        out_shape=(jax.ShapeDtypeStruct((columns, depth), BF16), jax.ShapeDtypeStruct((1,), I32)),
        in_specs=[SMEM, SMEM, SMEM, VMEM, pl.BlockSpec((a_rows, slab_count, step), lambda p: (0, 0, p))],
        out_specs=(pl.BlockSpec((columns, LANES), lambda p: (0, p)), SMEM),
        compiler_params=params(),
        name="squeeze_amp",
    )(irrep_virt, irrep_occ, irrep_slab, labels, amplitudes)

    def rest(slots, virt, occ, slab, labels, own, other, amp_small):
        parts = pl.pallas_call(
            functools.partial(multiply_kernel, slots, va_axes),
            out_shape=jax.ShapeDtypeStruct((chips, slots, columns), F32),
            in_specs=[SMEM, SMEM, SMEM] + [VMEM] * 4,
            out_specs=VMEM,
            scratch_shapes=[pltpu.VMEM((chips * WINDOW, depth), BF16), pltpu.VMEM((chips * WINDOW, LANES), I32)],
            compiler_params=params(),
            name="multiply",
        )(virt, occ, slab, labels, own, other, amp_small)
        parts = lax.all_to_all(parts, ("xh", "z"), 0, 0, tiled=False)
        return pl.pallas_call(
            functools.partial(finish_kernel, slots, va_axes, vb_axes),
            out_shape=jax.ShapeDtypeStruct((WINDOW, columns), BF16),
            in_specs=[SMEM, SMEM, SMEM] + [VMEM] * 2,
            out_specs=VMEM,
            compiler_params=params(),
            name="finish",
        )(virt, occ, slab, labels, parts)

    return lax.cond(
        most[0] <= SLOTS,
        functools.partial(rest, SLOTS),
        functools.partial(rest, WINDOW),
        irrep_virt, irrep_occ, irrep_slab, labels, own, other, amp_small,
    )


def solution(mesh):
    names = ("xl", "y", "c", "xh", "z")
    shape = (2, mesh.shape["va"] // 4, 2, 2, mesh.shape["vb"] // 2)
    fine = Mesh(mesh.devices.reshape(shape), names)
    va, vb = names[:3], names[3:]
    return jax.shard_map(
        functools.partial(per_device, dict(zip(names, shape))),
        mesh=fine,
        in_specs=(P(va, None, vb), P(va, vb), P(), P(), P()),
        out_specs=P(vb, va),
        check_vma=False,
    )
```

time: 311 us -> 64 us (0.21)
  waiting for transfers between devices: 283 us -> 0.01 us
  blocking collectives: 0 us -> 50.7 us
  between operations: 13.4 us -> 0.73 us
  matrix products: 7.99 us -> 0 us
  Pallas kernels: 0 us -> 7.17 us
  other arithmetic: 4.25 us -> 0 us
    reduce_scatter x1 -> x0, waiting for transfers between devices: 206 us -> none  [per_device(): lax.psum_scatter(lax.dot_general(int_sym, flat_amp, (((1,), (1,)), ((), (...]
    all_gather x1 -> x0, waiting for transfers between devices: 76.8 us -> none  [per_device(): gathered = lax.all_gather(integrals, 'va', axis=0, tiled=True)]
    all_to_all x0 -> x2, blocking collectives: none -> 50.7 us  [the longest x1 27.5 us: rest(): parts = lax.all_to_all(parts, ('xh', 'z'), 0, 0, tiled=False)]
    dot_general x1 -> x0, matrix products: 7.99 us -> none  [per_device(): lax.dot_general(int_sym, flat_amp, (((1,), (1,)), ((), ())), preferred_el...]
    pallas_call x0 -> x4, Pallas kernels: none -> 7.17 us  [the longest x1 3.13 us: per_device(): pl.pallas_call(functools.partial(squeeze_amp_kernel, va_axes, vb_axes), g...]
    unnamed x0 -> x12, local copies, waits for them, and re-layouts: none -> 3.16 us
  transfers between devices with their start and end apart: 2 -> 1, of which waited for: 2 -> 0; matrix products, arithmetic and copies ran while one was open for 1% -> 0% of each run, Pallas kernels for 0% -> 5%
where the time goes in v1:
time: 64 us; the launch traced here: 63.7 us
  blocking collectives  50.7 us (79%)
  Pallas kernels  7.17 us (11%)
  local copies, waits for them, and re-layouts  3.16 us (5%)
  starting transfers between devices  1.91 us (3%)
  between operations  0.73 us (1%)
    all_to_all x1, blocking collectives, rest(): parts = lax.all_to_all(parts, ('xh', 'z'), 0, 0, tiled=False)  27.5 us
    all_to_all x1, blocking collectives, per_device(): own = lax.all_to_all(small, ('xl', 'y'), 0, 0, tiled=False)  23.3 us
    unnamed x12, local copies, waits for them, and re-layouts  3.16 us
    pallas_call x1, Pallas kernels, per_device(): pl.pallas_call(functools.partial(squeeze_amp_kernel, va_axes, vb_axes), g...  3.13 us
    ppermute x1, starting transfers between devices, per_device(): other = lax.ppermute(own, 'c', [(0, 1), (1, 0)])  1.91 us
    pallas_call x1, Pallas kernels, rest(): pl.pallas_call(functools.partial(multiply_kernel, slots, va_axes), out_sh...  1.9 us
  transfers between devices with their start and end apart: 1, of which 0 were waited for; matrix products, arithmetic and copies ran while one was open for 0% of the time, Pallas kernels for 5%

profile of v1, /device:TPU:8, one launch (start us, length us, event | category | flops | bytes accessed | tf_op | source)
XLA Modules:
  0.0 63.7 jit_solution(8643544010518962991)
XLA Ops:
  0.0 0.0 copy-start.1
  0.0 0.9 %copy-done.1 = bf16[32,4096]{1,0:T(8,128)(2,1)S(1)} copy-done((bf16[32,4096]{1,0:T(8,128)(2,1)S(1)}, bf16[32,4096]{1,0:T(8,128)(2,1)}, u32[]{:S(2)}) %copy-start.1) | copy-done | bytes 262168
  1.0 0.0 copy-start.2
  1.0 0.0 copy-start.4
  1.0 0.0 copy-start.5
  1.0 1.2 %squeeze_int.1 = bf16[16,32,512]{2,1,0:T(8,128)(2,1)S(1)} custom-call(s32[1024]{0:T(1024)} %virt_ref.3, s32[64]{0:T(128)} %occ_ref.3, bf16[32,4096]{1,0:T(8,128)(2,1)S(1)} %copy-done.1), custom_call_target="tpu_custom_call" | custom-call | tf_op jit(solution)/shard_map/squeeze_int/pallas_call | solution.py:201
  2.2 23.3 %all_to_all.15 = bf16[16,32,512]{2,1,0:T(8,128)(2,1)S(1)} all-to-all(bf16[16,32,512]{2,1,0:T(8,128)(2,1)S(1)} %squeeze_int.1), channel_id=1, replica_groups=mesh['xl'=2,'y'=8,'c'=2,'xh'=2,'z'=8] {'xl','y'}, dimensions={0} | all-to-all | bytes 1048576 | tf_op jit(solution)/shard_map/all_to_all | solution.py:209
  25.4 1.9 %collective-permute-start = (bf16[16,32,512]{2,1,0:T(8,128)(2,1)S(1)}, bf16[16,32,512]{2,1,0:T(8,128)(2,1)S(1)}, u32[]{:S(2)}, u32[]{:S(2)}) collective-permute-start(bf16[16,32,512]{2,1,0:T(8,128)(2,1)S(1)} %all_to_all.15), channel_id=1, source_target_pairs={{0,16},{16,0},{1,17},{17,1},{2,18},{18,2},{3,19},{19,3},{4,20},{20... | collective-permute-start | bytes 1572872 | tf_op jit(solution)/shard_map/ppermute | solution.py:210
  27.4 0.0 copy-start
  27.4 1.6 %copy-done = bf16[32,8,4096]{2,1,0:T(8,128)(2,1)S(1)} copy-done((bf16[32,8,4096]{2,1,0:T(8,128)(2,1)S(1)}, bf16[32,8,4096]{2,1,0:T(8,128)(2,1)}, u32[]{:S(2)}) %copy-start) | copy-done | bytes 2097176
  29.0 3.1 %squeeze_amp.1 = (bf16[256,512]{1,0:T(8,128)(2,1)S(1)}, s32[1]{0:T(128)}) custom-call(s32[1024]{0:T(1024)} %virt_ref.3, s32[64]{0:T(128)} %occ_ref.3, s32[8]{0:T(128)} %slab_ref.1, s32[8,128]{1,0:T(8,128)} %bitcast.2, bf16[32,8,4096]{2,1,0:T(8,128)(2,1)S(1)} %copy-done), custom_call_target="tpu_custom_call" | custom-call | tf_op jit(solution)/shard_map/squeeze_amp/pallas_call | solution.py:213
  32.7 0.0 collective-permute-done
  32.8 0.0 copy-done.2
  32.8 0.0 copy-done.4
  32.8 0.0 copy-done.5
  32.8 30.3 %conditional.1 = (bf16[64,256]{1,0:T(8,128)(2,1)S(1)}) conditional(s32[]{:T(128)} %bitcast.1, (s32[1024]{0:T(1024)S(1)}, s32[64]{0:T(128)S(1)}, s32[8]{0:T(128)S(1)}, s32[8,128]{1,0:T(8,128)S(1)}, bf16[16,32,512]{2,1,0:T(8,128)(2,1)S(1)}, /*index=5*/bf16[16,32,512]{2,1,0:T(8,128)(2,1)S(1)}, bf16[256,512]{1,0:T(8,128)(2,1)S(1)}) %tuple.23, ...), branch_computations={%region_0.0_spmd, %region_1.0_spmd} | conditional | bytes 2097160 | solution.py:243
  32.8 1.9 %multiply.3 = f32[16,24,256]{2,1,0:T(8,128)S(1)} custom-call(s32[1024]{0:T(1024)S(1)} %bitcast.7, s32[64]{0:T(128)S(1)} %get-tuple-element.44.occ_ref, s32[8]{0:T(128)S(1)} %get-tuple-element.45.slab_ref, s32[8,128]{1,0:T(8,128)S(1)} %get-tuple-element.46.labels_ref, bf16[16,32,512]{2,1,0:T(8,128)(2,1)S(1)} %get-tuple-element.47.own_ref, ...), custom_call_target="tpu_custom_call" | custom-call | tf_op jit(solution)/shard_map/cond/branch_1_fun/multiply/pallas_call | solution.py:224
  34.7 27.5 %all_to_all.14.parts_ref = f32[16,24,256]{2,1,0:T(8,128)S(1)} all-to-all(f32[16,24,256]{2,1,0:T(8,128)S(1)} %multiply.3), channel_id=1, replica_groups=mesh['xl'=2,'y'=8,'c'=2,'xh'=2,'z'=8] {'xh','z'}, dimensions={0} | all-to-all | bytes 786432 | tf_op jit(solution)/shard_map/cond/branch_1_fun/all_to_all | solution.py:233
  62.2 0.9 %finish.3 = bf16[64,256]{1,0:T(8,128)(2,1)S(1)} custom-call(s32[1024]{0:T(1024)S(1)} %bitcast.8, s32[64]{0:T(128)S(1)} %get-tuple-element.44.occ_ref, s32[8]{0:T(128)S(1)} %get-tuple-element.45.slab_ref, s32[8,128]{1,0:T(8,128)S(1)} %get-tuple-element.46.labels_ref, f32[16,24,256]{2,1,0:T(8,128)S(1)} %all_to_all.14.parts_ref), custom_call_target="tpu_custom_call" | custom-call | tf_op jit(solution)/shard_map/cond/branch_1_fun/finish/pallas_call | solution.py:234
  63.1 0.0 copy-start.3
  63.1 0.6 copy-done.3
Async XLA Ops:
  0.0 0.9 %copy-start.1 = (bf16[32,4096]{1,0:T(8,128)(2,1)S(1)}, bf16[32,4096]{1,0:T(8,128)(2,1)}, u32[]{:S(2)}) copy-start(bf16[32,4096]{1,0:T(8,128)(2,1)} %int_ref.1) | copy-start | bytes 786436
  1.0 31.8 %copy-start.2 = (s32[1024]{0:T(1024)S(1)}, s32[1024]{0:T(1024)}, u32[]{:S(2)}) copy-start(s32[1024]{0:T(1024)} %virt_ref.3) | copy-start | bytes 12292
  1.0 31.8 %copy-start.4 = (s32[64]{0:T(128)S(1)}, s32[64]{0:T(128)}, u32[]{:S(2)}) copy-start(s32[64]{0:T(128)} %occ_ref.3) | copy-start | bytes 772
  1.0 31.8 %copy-start.5 = (s32[8]{0:T(128)S(1)}, s32[8]{0:T(128)}, u32[]{:S(2)}) copy-start(s32[8]{0:T(128)} %slab_ref.1) | copy-start | bytes 100
  25.4 7.3 %collective-permute-start = (bf16[16,32,512]{2,1,0:T(8,128)(2,1)S(1)}, bf16[16,32,512]{2,1,0:T(8,128)(2,1)S(1)}, u32[]{:S(2)}, u32[]{:S(2)}) collective-permute-start(bf16[16,32,512]{2,1,0:T(8,128)(2,1)S(1)} %all_to_all.15), channel_id=1, source_target_pairs={{0,16},{16,0},{1,17},{17,1},{2,18},{18,2},{3,19},{19,3},{4,20},{20... | collective-permute-start | bytes 1572872 | tf_op jit(solution)/shard_map/ppermute | solution.py:210
  27.4 1.6 %copy-start = (bf16[32,8,4096]{2,1,0:T(8,128)(2,1)S(1)}, bf16[32,8,4096]{2,1,0:T(8,128)(2,1)}, u32[]{:S(2)}) copy-start(bf16[32,8,4096]{2,1,0:T(8,128)(2,1)} %amp_ref.1) | copy-start | bytes 6291460
  63.1 0.6 copy-start.3

commit v2 on v1

v2 whole, which is shorter than its diff:
```python
import functools

import jax
import jax.numpy as jnp
from jax import lax
from jax.experimental import pallas as pl
from jax.experimental.pallas import tpu as pltpu
from jax.sharding import Mesh, PartitionSpec as P

GROUP = 8
LANES = 128
ROOTS = 4
TOP = 7.0
SMALLEST = 2.0**-100
WINDOW = 64
SLOTS = 24

F32, BF16, I32 = jnp.float32, jnp.bfloat16, jnp.int32
SMEM = pl.BlockSpec(memory_space=pltpu.SMEM)
VMEM = pl.BlockSpec(memory_space=pltpu.VMEM)
HBM = pl.BlockSpec(memory_space=pltpu.HBM)
ANY = pl.BlockSpec(memory_space=pl.ANY)


def params(**more):
    return pltpu.CompilerParams(vmem_limit_bytes=48 << 20, **more)


def lanes(shape):
    return lax.broadcasted_iota(I32, shape, len(shape) - 1)


def rows_of(shape):
    return lax.broadcasted_iota(I32, shape, len(shape) - 2)


def spread(ref, start, count, position):
    out = jnp.zeros_like(position)
    for n in range(count):
        out = jnp.where(position == n, ref[start + n], out)
    return out


def occ_lanes(occ_ref):
    occ_count = occ_ref.shape[0]
    return spread(occ_ref, 0, occ_count, lanes((1, LANES)) % occ_count)


def pair_tags(occ, virt_ref, first_c, block, occ_count):
    per = LANES // occ_count
    c_of = lanes((1, LANES)) // occ_count
    return occ ^ spread(virt_ref, first_c + block * per, per, c_of)


def squeezer(width):
    shape = (width, width // GROUP)
    return jnp.where(rows_of(shape) // GROUP == lanes(shape), 1.0, 0.0).astype(BF16)


def first_of(axis_sizes):
    at = 0
    for name, size in axis_sizes:
        at = at * size + lax.axis_index(name)
    return at


def squeeze_int_kernel(va_axes, vb_axes, virt_hbm, occ_hbm, int_hbm, out_hbm, virt_ref, occ_ref, int_ref, small_ref, sems):
    row_count, width = int_ref.shape
    occ_count = occ_ref.shape[0]
    c_count = width // occ_count
    step = GROUP * LANES
    parts = width // step
    fetch = [
        pltpu.make_async_copy(virt_hbm, virt_ref, sems.at[0]),
        pltpu.make_async_copy(occ_hbm, occ_ref, sems.at[1]),
    ]
    for part in range(parts):
        span = pl.ds(part * step, step)
        fetch.append(pltpu.make_async_copy(int_hbm.at[:, span], int_ref.at[:, span], sems.at[2 + part]))
    for copy in fetch:
        copy.start()
    va, vb = first_of(va_axes), first_of(vb_axes)
    squeeze = squeezer(step)
    fetch[0].wait()
    fetch[1].wait()
    occ = occ_lanes(occ_ref)
    row_tag = spread(virt_ref, va * row_count, row_count, rows_of((row_count, LANES))) ^ occ_ref[0]
    for part in range(parts):
        fetch[2 + part].wait()
        kept = []
        for block in range(GROUP):
            at = part * GROUP + block
            tag = pair_tags(occ, virt_ref, vb * c_count, at, occ_count)
            held = int_ref[:, at * LANES : (at + 1) * LANES].astype(F32)
            kept.append(jnp.where(row_tag == tag, held, 0.0).astype(BF16))
        small = jnp.dot(jnp.concatenate(kept, 1), squeeze, preferred_element_type=F32)
        small_ref[:, part * LANES : (part + 1) * LANES] = small.astype(BF16)
    peers = out_hbm.shape[0]
    copies = [pltpu.make_async_copy(small_ref, out_hbm.at[peer], sems.at[2 + parts + peer]) for peer in range(peers)]
    for copy in copies:
        copy.start()
    for copy in copies:
        copy.wait()


def squeeze_amp_kernel(va_axes, vb_axes, virt_ref, occ_ref, slab_ref, amp_ref, out_ref):
    row_count, width = amp_ref.shape
    occ_count, slab_count = occ_ref.shape[0], slab_ref.shape[0]
    va, vb = first_of(va_axes), first_of(vb_axes)
    occ = occ_lanes(occ_ref)
    slab = spread(slab_ref, 0, slab_count, rows_of((slab_count, LANES)))
    a_count = row_count // slab_count
    left = jnp.concatenate([slab ^ virt_ref[va * a_count + a] for a in range(a_count)], 0)
    step = GROUP * LANES
    squeeze = squeezer(step)
    for part in range(width // step):
        kept = []
        for block in range(GROUP):
            at = part * GROUP + block
            tag = pair_tags(occ, virt_ref, vb * (width // occ_count), at, occ_count)
            held = amp_ref[:, at * LANES : (at + 1) * LANES].astype(F32)
            kept.append(jnp.where(left == tag, held, 0.0).astype(BF16))
        small = jnp.dot(jnp.concatenate(kept, 1), squeeze, preferred_element_type=F32)
        out_ref[:, part * LANES : (part + 1) * LANES] = small.astype(BF16)


def sort_keys(labels):
    at = lanes(labels.shape)
    return (at // WINDOW) * (WINDOW * GROUP) + labels * WINDOW + at % WINDOW


def column_tags(va_axes, virt_ref, slab_ref, occ_ref, a_count):
    slab_count = slab_ref.shape[0]
    at = lanes((1, a_count * slab_count))
    first = spread(virt_ref, first_of(va_axes) * a_count, a_count, at // slab_count)
    return first ^ spread(slab_ref, 0, slab_count, at % slab_count) ^ occ_ref[0]


def plan_kernel(
    half_rows, va_axes, vb_axes, virt_ref, occ_ref, slab_ref, labels_ref,
    move_ref, tag_ref, columns_ref, place_ref, label_ref, most_ref,
):
    core = lax.axis_index("c")
    columns = column_tags(va_axes, virt_ref, slab_ref, occ_ref, half_rows)
    columns_ref[...] = jnp.broadcast_to(columns, columns_ref.shape)
    labels = labels_ref[...]
    half = lanes(labels.shape) // WINDOW
    most = jnp.int32(0)
    for label in range(GROUP):
        for side in range(LANES // WINDOW):
            hits = jnp.where((labels == label) & (half == side), 1.0, 0.0)
            most = jnp.maximum(most, jnp.max(jnp.sum(hits, axis=1, keepdims=True)).astype(I32))
    most_ref[0] = most

    keys = sort_keys(labels)
    keys_down = jnp.transpose(keys.astype(F32))
    swap = (lanes(keys.shape) // half_rows) % 2 == 0

    def own_first(x):
        x = x.astype(F32)
        swapped = jnp.where(swap, pltpu.roll(x, LANES - half_rows, 1), pltpu.roll(x, half_rows, 1))
        return jnp.where(core == 0, x, swapped)

    keys_across, labels_across = own_first(keys), own_first(labels)
    square = (LANES, LANES)
    for r in range(labels.shape[0]):
        before = jnp.where(keys_down[:, r : r + 1] < keys_across[r : r + 1, :], 1.0, 0.0)
        place = jnp.sum(before, axis=0, keepdims=True)
        moved = jnp.where(rows_of(square).astype(F32) == place, 1.0, 0.0)
        move_ref[r] = moved.astype(BF16)
        tag_ref[r * LANES : (r + 1) * LANES, :] = jnp.broadcast_to(
            jnp.sum(moved * labels_across[r : r + 1, :], axis=1, keepdims=True), square
        ).astype(I32)

    vb, per = first_of(vb_axes), LANES // WINDOW
    row = labels_ref[pl.ds(vb // per, 1), :]
    mine = lanes(row.shape) // WINDOW == vb % per
    key = jnp.where(mine, row * WINDOW + lanes(row.shape) % WINDOW, WINDOW * GROUP).astype(F32)
    own = jnp.where(mine, lanes(row.shape) % WINDOW, -1)
    on_own = rows_of(place_ref.shape) == own
    key_down = jnp.sum(jnp.where(on_own, key, 0.0), axis=1, keepdims=True)
    label_down = jnp.sum(jnp.where(on_own, row.astype(F32), 0.0), axis=1, keepdims=True)
    label_ref[...] = jnp.broadcast_to(label_down, label_ref.shape).astype(I32)
    place = jnp.sum(jnp.where(key < key_down, 1.0, 0.0), axis=1, keepdims=True)
    place_ref[...] = jnp.broadcast_to(place, place_ref.shape).astype(I32)


def multiply_kernel(slots, move_ref, tag_ref, columns_ref, own_ref, other_ref, amp_ref, out_ref, sorted_ref):
    windows = own_ref.shape[0]
    per = LANES // WINDOW
    halves = amp_ref.shape[0] // LANES
    for r in range(windows // per):
        block = jnp.concatenate([x for w in range(r * per, (r + 1) * per) for x in (own_ref[w], other_ref[w])], 0)
        span = slice(r * LANES, (r + 1) * LANES)
        sorted_ref[span, :] = jnp.dot(move_ref[r], block, preferred_element_type=F32).astype(BF16)
    for r in range(windows // per):
        span = slice(r * LANES, (r + 1) * LANES)
        sums = lax.dot_general(
            sorted_ref[span, :], amp_ref[...], (((1,), (1,)), ((), ())), preferred_element_type=F32
        )
        tags = jnp.concatenate([tag_ref[span, :]] * halves, 1)
        sums = jnp.where(tags == columns_ref[0:1, :], sums, 0.0)
        for w in range(per):
            part = sums[w * WINDOW : (w + 1) * WINDOW]
            total = part[:slots]
            for low in range(slots, WINDOW, slots):
                more = part[low : low + slots]
                if more.shape[0] < slots:
                    more = jnp.concatenate([more, jnp.zeros((slots - more.shape[0], more.shape[1]), F32)], 0)
                total = total + more
            largest = jnp.max(jnp.max(jnp.abs(total), axis=0, keepdims=True), axis=1, keepdims=True)
            power = jnp.ceil(jnp.log2(jnp.maximum(largest, SMALLEST)))
            total = total * jnp.exp2(TOP - power)
            code = total * jnp.abs(total)
            square = total * total
            for _ in range(ROOTS - 1):
                code, square = code * square, square * square
            code = code.astype(BF16)
            for half in range(halves):
                out_ref[r * per + w, half * slots : (half + 1) * slots, :] = code[:, half * LANES : (half + 1) * LANES]
            out_ref[r * per + w, halves * slots :, :] = jnp.broadcast_to(power, (GROUP, LANES)).astype(BF16)


def finish_kernel(slots, columns_ref, place_ref, label_ref, parts_ref, out_ref):
    halves = out_ref.shape[1] // LANES
    total = jnp.zeros((halves * slots, LANES), F32)
    for part in range(parts_ref.shape[0]):
        power = parts_ref[part, halves * slots :, :].astype(F32)
        code = parts_ref[part, : halves * slots, :].astype(F32)
        root = jnp.abs(code)
        for _ in range(ROOTS):
            root = jnp.sqrt(root)
        total = total + jnp.where(code < 0.0, -root, root) * jnp.exp2(power[0:1, :] - TOP)
    total = jnp.concatenate([total[half * slots : (half + 1) * slots] for half in range(halves)], 1)
    place = place_ref[:, 0:1]
    slot = jnp.where(place >= 2 * slots, place - 2 * slots, jnp.where(place >= slots, place - slots, place))
    chosen = jnp.where(lanes((WINDOW, slots)) == slot, 1.0, 0.0).astype(BF16)
    full = jnp.dot(chosen, total.astype(BF16), preferred_element_type=F32)
    out_ref[...] = jnp.where(label_ref[...] == columns_ref[0:1, :], full, 0.0).astype(BF16)


def per_device(sizes, amplitudes, integrals, irrep_virt, irrep_occ, irrep_slab):
    va_axes = [(name, sizes[name]) for name in ("xl", "y", "c")]
    vb_axes = [(name, sizes[name]) for name in ("xh", "z")]
    a_rows, slab_count, width = amplitudes.shape
    b_rows = integrals.shape[0]
    depth = width // GROUP
    chips = sizes["xl"] * sizes["y"]
    labels = irrep_virt.reshape(-1, LANES)
    columns = a_rows * slab_count
    shaped = jax.ShapeDtypeStruct

    small = pl.pallas_call(
        functools.partial(squeeze_int_kernel, va_axes, vb_axes),
        out_shape=shaped((chips, b_rows, depth), BF16),
        in_specs=[HBM] * 3,
        out_specs=ANY,
        scratch_shapes=[
            pltpu.SMEM(irrep_virt.shape, I32),
            pltpu.SMEM(irrep_occ.shape, I32),
            pltpu.VMEM((b_rows, width), BF16),
            pltpu.VMEM((b_rows, depth), BF16),
            pltpu.SemaphoreType.DMA((2 + width // (GROUP * LANES) + chips,)),
        ],
        compiler_params=params(),
        name="squeeze_int",
    )(*(pltpu.with_memory_space_constraint(x, pltpu.HBM) for x in (irrep_virt, irrep_occ, integrals)))
    own = lax.all_to_all(small, ("xl", "y"), 0, 0, tiled=False)

    amp_small = pl.pallas_call(
        functools.partial(squeeze_amp_kernel, va_axes, vb_axes),
        out_shape=shaped((columns, depth), BF16),
        in_specs=[SMEM, SMEM, SMEM, VMEM],
        out_specs=VMEM,
        compiler_params=params(),
        cost_estimate=pl.CostEstimate(flops=4 << 30, transcendentals=0, bytes_accessed=8 << 20),
        name="squeeze_amp",
    )(irrep_virt, irrep_occ, irrep_slab, amplitudes.reshape(columns, width))

    *plan, most = pl.pallas_call(
        functools.partial(plan_kernel, b_rows, va_axes, vb_axes),
        out_shape=(
            shaped((labels.shape[0], LANES, LANES), BF16),
            shaped((labels.size, LANES), I32),
            shaped((8, columns), I32),
            shaped((WINDOW, LANES), I32),
            shaped((WINDOW, columns), I32),
            shaped((1,), I32),
        ),
        in_specs=[SMEM, SMEM, SMEM, VMEM],
        out_specs=(VMEM,) * 5 + (SMEM,),
        compiler_params=params(),
        cost_estimate=pl.CostEstimate(flops=2 << 30, transcendentals=0, bytes_accessed=4 << 20),
        name="plan",
    )(irrep_virt, irrep_occ, irrep_slab, labels)

    own, amp_small, most, *plan = lax.optimization_barrier((own, amp_small, most, *plan))
    other = lax.ppermute(own, "c", [(0, 1), (1, 0)])

    def rest(slots, move, tags, column_labels, place, row_labels, own, other, amp_small):
        sent_rows = columns // LANES * slots + GROUP
        parts = pl.pallas_call(
            functools.partial(multiply_kernel, slots),
            out_shape=shaped((chips, sent_rows, LANES), BF16),
            in_specs=[VMEM] * 6,
            out_specs=VMEM,
            scratch_shapes=[pltpu.VMEM((chips * WINDOW, depth), BF16)],
            compiler_params=params(),
            name="multiply",
        )(move, tags, column_labels, own, other, amp_small)
        parts = lax.all_to_all(parts, ("xh", "z"), 0, 0, tiled=False)
        return pl.pallas_call(
            functools.partial(finish_kernel, slots),
            out_shape=shaped((WINDOW, columns), BF16),
            in_specs=[VMEM] * 4,
            out_specs=VMEM,
            compiler_params=params(),
            name="finish",
        )(column_labels, place, row_labels, parts)

    return lax.cond(
        most[0] <= SLOTS,
        functools.partial(rest, SLOTS),
        functools.partial(rest, WINDOW),
        *plan, own, other, amp_small,
    )


def solution(mesh):
    names = ("xl", "y", "c", "xh", "z")
    shape = (2, mesh.shape["va"] // 4, 2, 2, mesh.shape["vb"] // 2)
    fine = Mesh(mesh.devices.reshape(shape), names)
    va, vb = names[:3], names[3:]
    return jax.shard_map(
        functools.partial(per_device, dict(zip(names, shape))),
        mesh=fine,
        in_specs=(P(va, None, vb), P(va, vb), P(), P(), P()),
        out_specs=P(vb, va),
        check_vma=False,
    )
```

time: 64 us -> 56.2 us (0.88)
  blocking collectives: 50.7 us -> 23.4 us
  waiting for transfers between devices: 0.01 us -> 10.5 us
  starting transfers between devices: 1.91 us -> 11.1 us
    all_to_all x1 -> x0, blocking collectives: 23.3 us -> none  [per_device(): own = lax.all_to_all(small, ('xl', 'y'), 0, 0, tiled=False)]
    all_to_all x0 -> x1, waiting for transfers between devices: none -> 9.3 us  [per_device(): own = lax.all_to_all(small, ('xl', 'y'), 0, 0, tiled=False)]
    all_to_all x0 -> x1, starting transfers between devices: none -> 9.2 us  [per_device(): own = lax.all_to_all(small, ('xl', 'y'), 0, 0, tiled=False)]
    all_to_all x1, blocking collectives: 27.5 us -> 23.4 us  [rest(): parts = lax.all_to_all(parts, ('xh', 'z'), 0, 0, tiled=False)]
    pallas_call x1, Pallas kernels: 1.22 us -> 2.5 us  [per_device(): pl.pallas_call(functools.partial(squeeze_int_kernel, va_axes, vb_axes), o...]
    ppermute x1, waiting for transfers between devices: 0.01 us -> 1.23 us  [per_device(): other = lax.ppermute(own, 'c', [(0, 1), (1, 0)])]
    pallas_call x3 -> x4, Pallas kernels: 5.95 us -> 4.95 us  [the longest x1 1.72 us: per_device(): pl.pallas_call(functools.partial(plan_kernel, b_rows, va_axes, vb_axes),...]
    unnamed x12 -> x10, local copies, waits for them, and re-layouts: 3.16 us -> 2.61 us
  transfers between devices with their start and end apart: 1 -> 2, of which waited for: 0 -> 2; matrix products, arithmetic and copies ran while one was open for 0% -> 0% of each run, Pallas kernels for 5% -> 6%
where the time goes in v2:
time: 56.2 us; the launch traced here: 55.8 us
  blocking collectives  23.4 us (42%)
  starting transfers between devices  11.1 us (20%)
  waiting for transfers between devices  10.5 us (19%)
  Pallas kernels  7.45 us (13%)
  local copies, waits for them, and re-layouts  2.61 us (5%)
  between operations  0.7 us (1%)
    all_to_all x1, blocking collectives, rest(): parts = lax.all_to_all(parts, ('xh', 'z'), 0, 0, tiled=False)  23.4 us
    all_to_all x1, waiting for transfers between devices, per_device(): own = lax.all_to_all(small, ('xl', 'y'), 0, 0, tiled=False)  9.3 us
    all_to_all x1, starting transfers between devices, per_device(): own = lax.all_to_all(small, ('xl', 'y'), 0, 0, tiled=False)  9.2 us
    unnamed x10, local copies, waits for them, and re-layouts  2.61 us
    pallas_call x1, Pallas kernels, per_device(): pl.pallas_call(functools.partial(squeeze_int_kernel, va_axes, vb_axes), o...  2.5 us
    ppermute x1, starting transfers between devices, per_device(): other = lax.ppermute(own, 'c', [(0, 1), (1, 0)])  1.91 us
    pallas_call x1, Pallas kernels, per_device(): pl.pallas_call(functools.partial(plan_kernel, b_rows, va_axes, vb_axes),...  1.72 us
    pallas_call x1, Pallas kernels, per_device(): pl.pallas_call(functools.partial(squeeze_amp_kernel, va_axes, vb_axes), o...  1.38 us
  transfers between devices with their start and end apart: 2, of which 2 were waited for; matrix products, arithmetic and copies ran while one was open for 0% of the time, Pallas kernels for 6%

profile of v2, /device:TPU:8, one launch (start us, length us, event | category | flops | bytes accessed | tf_op | source)
XLA Modules:
  0.0 55.8 jit_solution(2458563495747258564)
XLA Ops:
  0.0 2.5 %squeeze_int.1 = bf16[16,32,512]{2,1,0:T(8,128)(2,1)} custom-call(s32[1024]{0:T(1024)} %virt_ref.3, s32[64]{0:T(128)} %occ_ref.3, bf16[32,4096]{1,0:T(8,128)(2,1)} %int_hbm.1), custom_call_target="tpu_custom_call" | custom-call | tf_op jit(solution)/shard_map/squeeze_int/pallas_call | solution.py:253
  2.5 9.2 %all-to-all-start.2 = ((bf16[16,32,512]{2,1,0:T(8,128)(2,1)}), bf16[16,32,512]{2,1,0:T(8,128)(2,1)S(1)}, u32[]{:S(2)}, u32[]{:S(2)}) async-start(bf16[16,32,512]{2,1,0:T(8,128)(2,1)} %squeeze_int.1), calls=%async_computation.2 | async-start | bytes 1048576 | tf_op jit(solution)/shard_map/all_to_all | solution.py:268
  11.7 0.0 copy-start
  11.7 0.7 %copy-done = s32[1024]{0:T(1024)S(1)} copy-done((s32[1024]{0:T(1024)S(1)}, s32[1024]{0:T(1024)}, u32[]{:S(2)}) %copy-start) | copy-done | bytes 4120
  12.4 0.0 copy-start.1
  12.4 0.7 %copy-done.1 = s32[64]{0:T(128)S(1)} copy-done((s32[64]{0:T(128)S(1)}, s32[64]{0:T(128)}, u32[]{:S(2)}) %copy-start.1) | copy-done | bytes 280
  13.0 0.0 copy-start.3
  13.1 0.7 %copy-done.3 = s32[8]{0:T(128)S(1)} copy-done((s32[8]{0:T(128)S(1)}, s32[8]{0:T(128)}, u32[]{:S(2)}) %copy-start.3) | copy-done | bytes 56
  13.7 0.0 copy-start.2
  13.7 1.7 %plan.1 = (bf16[8,128,128]{2,1,0:T(8,128)(2,1)S(1)}, s32[1024,128]{1,0:T(8,128)S(1)}, s32[8,256]{1,0:T(8,128)S(1)}, s32[64,128]{1,0:T(8,128)S(1)}, s32[64,256]{1,0:T(8,128)S(1)}, /*index=5*/s32[1]{0:T(128)}) custom-call(s32[1024]{0:T(1024)S(1)} %copy-done, s32[64]{0:T(128)S(1)} %copy-done.1, s32[8]{0:T(128)S(1)} %copy-done.3, s32[8,128]{1,0:T(8,128)S(1)} %bitcast.3), custom_call_target="tpu_custom_call" | custom-call | flops 2147483648 | bytes 4194304 | tf_op jit(solution)/shard_map/plan/pallas_call | solution.py:280
  15.4 0.0 copy-done.2
  15.4 1.4 %squeeze_amp.1 = bf16[256,512]{1,0:T(8,128)(2,1)S(1)} custom-call(s32[1024]{0:T(1024)S(1)} %copy-done, s32[64]{0:T(128)S(1)} %copy-done.1, s32[8]{0:T(128)S(1)} %copy-done.3, bf16[256,4096]{1,0:T(8,128)(2,1)S(1)} %bitcast.4), custom_call_target="tpu_custom_call" | custom-call | flops 4294967296 | bytes 8388608 | tf_op jit(solution)/shard_map/squeeze_amp/pallas_call | solution.py:270
  16.8 9.3 %all-to-all-done.2 = bf16[16,32,512]{2,1,0:T(8,128)(2,1)S(1)} async-done(((bf16[16,32,512]{2,1,0:T(8,128)(2,1)}), bf16[16,32,512]{2,1,0:T(8,128)(2,1)S(1)}, u32[]{:S(2)}, u32[]{:S(2)}) %all-to-all-start.2) | async-done | bytes 524320 | tf_op jit(solution)/shard_map/all_to_all | solution.py:268
  26.1 1.9 %collective-permute-start = (bf16[16,32,512]{2,1,0:T(8,128)(2,1)S(1)}, bf16[16,32,512]{2,1,0:T(8,128)(2,1)S(1)}, u32[]{:S(2)}, u32[]{:S(2)}) collective-permute-start(bf16[16,32,512]{2,1,0:T(8,128)(2,1)S(1)} %all-to-all-done.2), channel_id=1, source_target_pairs={{0,16},{16,0},{1,17},{17,1},{2,18},{18,2},{3,19},{19,3},{4,20},{20... | collective-permute-start | bytes 1572872 | tf_op jit(solution)/shard_map/ppermute | solution.py:298
  28.7 1.2 %collective-permute-done = bf16[16,32,512]{2,1,0:T(8,128)(2,1)S(1)} collective-permute-done((bf16[16,32,512]{2,1,0:T(8,128)(2,1)S(1)}, bf16[16,32,512]{2,1,0:T(8,128)(2,1)S(1)}, u32[]{:S(2)}, u32[]{:S(2)}) %collective-permute-start) | collective-permute-done | bytes 524320 | tf_op jit(solution)/shard_map/ppermute | solution.py:298
  29.9 25.2 %conditional.1 = (bf16[64,256]{1,0:T(8,128)(2,1)S(1)}) conditional(s32[]{:T(128)} %bitcast.2, (bf16[8,128,128]{2,1,0:T(8,128)(2,1)S(1)}, s32[1024,128]{1,0:T(8,128)S(1)}, s32[8,256]{1,0:T(8,128)S(1)}, bf16[16,32,512]{2,1,0:T(8,128)(2,1)S(1)}, bf16[16,32,512]{2,1,0:T(8,128)(2,1)S(1)}, /*index=5*/bf16[256,512]{1,0:T(8,128)(2,1)S(1)}, ...), branch_computations={%region_0.0_spmd, %region_1.0_spmd} | conditional | bytes 1114120 | solution.py:321
  29.9 1.3 %multiply.3 = bf16[16,56,128]{2,1,0:T(8,128)(2,1)S(1)} custom-call(bf16[8,128,128]{2,1,0:T(8,128)(2,1)S(1)} %get-tuple-element.51.move_ref, s32[1024,128]{1,0:T(8,128)S(1)} %get-tuple-element.52.tag_ref, s32[8,256]{1,0:T(8,128)S(1)} %get-tuple-element.48.columns_ref, bf16[16,32,512]{2,1,0:T(8,128)(2,1)S(1)} %get-tuple-element.53.own_ref, ...), custom_call_target="tpu_custom_call" | custom-call | tf_op jit(solution)/shard_map/cond/branch_1_fun/multiply/pallas_call | solution.py:302
  31.2 23.4 %all_to_all.14.parts_ref = bf16[16,56,128]{2,1,0:T(8,128)(2,1)S(1)} all-to-all(bf16[16,56,128]{2,1,0:T(8,128)(2,1)S(1)} %multiply.3), channel_id=1, replica_groups=mesh['xl'=2,'y'=8,'c'=2,'xh'=2,'z'=8] {'xh','z'}, dimensions={0} | all-to-all | bytes 458752 | tf_op jit(solution)/shard_map/cond/branch_1_fun/all_to_all | solution.py:311
  54.5 0.6 %finish.3 = bf16[64,256]{1,0:T(8,128)(2,1)S(1)} custom-call(s32[8,256]{1,0:T(8,128)S(1)} %get-tuple-element.48.columns_ref, s32[64,128]{1,0:T(8,128)S(1)} %get-tuple-element.49.place_ref, s32[64,256]{1,0:T(8,128)S(1)} %get-tuple-element.50.label_ref, bf16[16,56,128]{2,1,0:T(8,128)(2,1)S(1)} %all_to_all.14.parts_ref), custom_call_target="tpu_custom_call" | custom-call | tf_op jit(solution)/shard_map/cond/branch_1_fun/finish/pallas_call | solution.py:312
  55.1 0.0 copy-start.4
  55.2 0.6 %copy-done.4 = bf16[64,256]{1,0:T(8,128)(2,1)} copy-done((bf16[64,256]{1,0:T(8,128)(2,1)}, bf16[64,256]{1,0:T(8,128)(2,1)S(1)}, u32[]{:S(2)}) %copy-start.4) | copy-done | bytes 32792
Async XLA Ops:
  2.5 23.6 %all-to-all-start.2 = ((bf16[16,32,512]{2,1,0:T(8,128)(2,1)}), bf16[16,32,512]{2,1,0:T(8,128)(2,1)S(1)}, u32[]{:S(2)}, u32[]{:S(2)}) async-start(bf16[16,32,512]{2,1,0:T(8,128)(2,1)} %squeeze_int.1), calls=%async_computation.2 | async-start | bytes 1048576 | tf_op jit(solution)/shard_map/all_to_all | solution.py:268
  11.7 0.7 %copy-start = (s32[1024]{0:T(1024)S(1)}, s32[1024]{0:T(1024)}, u32[]{:S(2)}) copy-start(s32[1024]{0:T(1024)} %virt_ref.3) | copy-start | bytes 12292
  12.4 0.7 %copy-start.1 = (s32[64]{0:T(128)S(1)}, s32[64]{0:T(128)}, u32[]{:S(2)}) copy-start(s32[64]{0:T(128)} %occ_ref.3) | copy-start | bytes 772
  13.0 0.7 %copy-start.3 = (s32[8]{0:T(128)S(1)}, s32[8]{0:T(128)}, u32[]{:S(2)}) copy-start(s32[8]{0:T(128)} %slab_ref.3) | copy-start | bytes 100
  13.7 1.7 %copy-start.2 = (bf16[32,8,4096]{2,1,0:T(8,128)(2,1)S(1)}, bf16[32,8,4096]{2,1,0:T(8,128)(2,1)}, u32[]{:S(2)}) copy-start(bf16[32,8,4096]{2,1,0:T(8,128)(2,1)} %param.7) | copy-start | bytes 6291460
  26.1 3.8 %collective-permute-start = (bf16[16,32,512]{2,1,0:T(8,128)(2,1)S(1)}, bf16[16,32,512]{2,1,0:T(8,128)(2,1)S(1)}, u32[]{:S(2)}, u32[]{:S(2)}) collective-permute-start(bf16[16,32,512]{2,1,0:T(8,128)(2,1)S(1)} %all-to-all-done.2), channel_id=1, source_target_pairs={{0,16},{16,0},{1,17},{17,1},{2,18},{18,2},{3,19},{19,3},{4,20},{20... | collective-permute-start | bytes 1572872 | tf_op jit(solution)/shard_map/ppermute | solution.py:298
  55.1 0.6 %copy-start.4 = (bf16[64,256]{1,0:T(8,128)(2,1)}, bf16[64,256]{1,0:T(8,128)(2,1)S(1)}, u32[]{:S(2)}) copy-start(bf16[64,256]{1,0:T(8,128)(2,1)S(1)} %get-tuple-element.90) | copy-start | bytes 98308

commit v3 on v2

v3 whole, which is shorter than its diff:
```python
import functools

import jax
import jax.numpy as jnp
from jax import lax
from jax.experimental import pallas as pl
from jax.experimental.pallas import tpu as pltpu
from jax.sharding import Mesh, PartitionSpec as P

GROUP = 8
LANES = 128
ROOTS = 4
TOP = 7.0
SMALLEST = 2.0**-100
WINDOW = 64
RUN = 32
SPAN = 16

F32, BF16, I32 = jnp.float32, jnp.bfloat16, jnp.int32
SMEM = pl.BlockSpec(memory_space=pltpu.SMEM)
VMEM = pl.BlockSpec(memory_space=pltpu.VMEM)
HBM = pl.BlockSpec(memory_space=pltpu.HBM)
ANY = pl.BlockSpec(memory_space=pl.ANY)


def params(**more):
    return pltpu.CompilerParams(vmem_limit_bytes=48 << 20, **more)


def lanes(shape):
    return lax.broadcasted_iota(I32, shape, len(shape) - 1)


def rows_of(shape):
    return lax.broadcasted_iota(I32, shape, len(shape) - 2)


def spread(ref, start, count, position):
    out = jnp.zeros_like(position)
    for n in range(count):
        out = jnp.where(position == n, ref[start + n], out)
    return out


def occ_lanes(occ_ref):
    occ_count = occ_ref.shape[0]
    return spread(occ_ref, 0, occ_count, lanes((1, LANES)) % occ_count)


def pair_tags(occ, virt_ref, first_c, block, occ_count):
    per = LANES // occ_count
    c_of = lanes((1, LANES)) // occ_count
    return occ ^ spread(virt_ref, first_c + block * per, per, c_of)


def squeezer(width):
    shape = (width, width // GROUP)
    return jnp.where(rows_of(shape) // GROUP == lanes(shape), 1.0, 0.0).astype(BF16)


def first_of(axis_sizes):
    at = 0
    for name, size in axis_sizes:
        at = at * size + lax.axis_index(name)
    return at


def squeeze_int_kernel(
    va_axes, vb_axes, virt_hbm, occ_hbm, slab_hbm, int_hbm, amp_hbm, out_hbm, amp_ref, pair_ref, left_ref,
    virt_ref, occ_ref, slab_ref, int_ref, small_ref, sems,
):
    row_count, width = int_ref.shape
    occ_count, slab_count = occ_ref.shape[0], slab_ref.shape[0]
    c_count = width // occ_count
    step = GROUP * LANES
    parts = width // step
    fetch = [
        pltpu.make_async_copy(virt_hbm, virt_ref, sems.at[0]),
        pltpu.make_async_copy(occ_hbm, occ_ref, sems.at[1]),
        pltpu.make_async_copy(slab_hbm, slab_ref, sems.at[2]),
    ]
    for part in range(parts):
        span = pl.ds(part * step, step)
        fetch.append(pltpu.make_async_copy(int_hbm.at[:, span], int_ref.at[:, span], sems.at[4 + part]))
    bring = pltpu.make_async_copy(amp_hbm, amp_ref, sems.at[3])
    for copy in fetch:
        copy.start()
    bring.start()
    va, vb = first_of(va_axes), first_of(vb_axes)
    squeeze = squeezer(step)
    for copy in fetch[:3]:
        copy.wait()
    occ = occ_lanes(occ_ref)
    row_tag = spread(virt_ref, va * row_count, row_count, rows_of((row_count, LANES))) ^ occ_ref[0]
    for part in range(parts):
        fetch[3 + part].wait()
        kept = []
        for block in range(GROUP):
            at = part * GROUP + block
            tag = pair_tags(occ, virt_ref, vb * c_count, at, occ_count)
            pair_ref[at : at + 1, :] = tag
            held = int_ref[:, at * LANES : (at + 1) * LANES].astype(F32)
            kept.append(jnp.where(row_tag == tag, held, 0.0).astype(BF16))
        small = jnp.dot(jnp.concatenate(kept, 1), squeeze, preferred_element_type=F32)
        small_ref[:, part * LANES : (part + 1) * LANES] = small.astype(BF16)
    peers, share = out_hbm.shape[0], out_hbm.shape[1]
    copies = []
    for peer in range(peers):
        part = peer // (peers * share // row_count)
        rows = small_ref.at[part * share : (part + 1) * share]
        copies.append(pltpu.make_async_copy(rows, out_hbm.at[peer], sems.at[4 + parts + peer]))
    for copy in copies:
        copy.start()
    slab = spread(slab_ref, 0, slab_count, rows_of((slab_count, LANES)))
    for a in range(row_count):
        left_ref[a * slab_count : (a + 1) * slab_count, :] = slab ^ virt_ref[va * row_count + a]
    for copy in copies:
        copy.wait()
    bring.wait()


def squeeze_amp_kernel(pair_ref, left_ref, amp_ref, out_ref):
    width = amp_ref.shape[1]
    left = left_ref[...]
    step = GROUP * LANES
    squeeze = squeezer(step)
    for part in range(width // step):
        kept = []
        for block in range(GROUP):
            at = part * GROUP + block
            held = amp_ref[:, at * LANES : (at + 1) * LANES].astype(F32)
            kept.append(jnp.where(left == pair_ref[at : at + 1, :], held, 0.0).astype(BF16))
        small = jnp.dot(jnp.concatenate(kept, 1), squeeze, preferred_element_type=F32)
        out_ref[:, part * LANES : (part + 1) * LANES] = small.astype(BF16)


def sort_keys(labels):
    at = lanes(labels.shape)
    return (at // RUN) * (RUN * GROUP) + labels * RUN + at % RUN


def column_tags(va, virt_ref, slab_ref, occ_ref, a_count):
    slab_count = slab_ref.shape[0]
    at = lanes((1, a_count * slab_count))
    first = spread(virt_ref, va * a_count, a_count, at // slab_count)
    return first ^ spread(slab_ref, 0, slab_count, at % slab_count) ^ occ_ref[0]


def plan_kernel(
    a_count, va_axes, vb_axes, virt_ref, occ_ref, slab_ref, labels_ref,
    move_ref, tag_ref, columns_ref, place_ref, label_ref, most_ref,
):
    core, share = lax.axis_index("c"), lax.axis_index("xl")
    va, vb = first_of(va_axes), first_of(vb_axes)
    across = va_axes[1][1] * va_axes[2][1]
    partner = va + (1 - 2 * share) * across
    for side, at in enumerate((va, partner)):
        tags = column_tags(at, virt_ref, slab_ref, occ_ref, a_count)
        columns_ref[8 * side : 8 * side + 8, :] = jnp.broadcast_to(tags, (8, tags.shape[1]))
    labels = labels_ref[...]
    run = lanes(labels.shape) // RUN
    most = jnp.int32(0)
    for label in range(GROUP):
        for side in range(LANES // RUN):
            hits = jnp.where((labels == label) & (run == side), 1.0, 0.0)
            most = jnp.maximum(most, jnp.max(jnp.sum(hits, axis=1, keepdims=True)).astype(I32))
    most_ref[0] = most

    count = labels.shape[0] // 2
    mine = jnp.where(share == 0, labels[:count], labels[count:])
    mine = jnp.concatenate([mine, mine], 0)
    keys = sort_keys(mine)
    keys_down = jnp.transpose(keys.astype(F32))
    half = RUN // 2
    swap = (lanes(keys.shape) // half) % 2 == 0

    def own_first(x):
        x = x.astype(F32)
        swapped = jnp.where(swap, pltpu.roll(x, LANES - half, 1), pltpu.roll(x, half, 1))
        return jnp.where(core == 0, x, swapped)

    keys_across, labels_across = own_first(keys), own_first(mine)
    square = (LANES, LANES)
    for r in range(count):
        before = jnp.where(keys_down[:, r : r + 1] < keys_across[r : r + 1, :], 1.0, 0.0)
        place = jnp.sum(before, axis=0, keepdims=True)
        moved = jnp.where(rows_of(square).astype(F32) == place, 1.0, 0.0)
        move_ref[r] = moved.astype(BF16)
        tag_ref[r * LANES : (r + 1) * LANES, :] = jnp.broadcast_to(
            jnp.sum(moved * labels_across[r : r + 1, :], axis=1, keepdims=True), square
        ).astype(I32)

    per = LANES // RUN
    for part in range(2):
        row = labels_ref[pl.ds(part * count + vb // per, 1), :]
        held = lanes(row.shape) // RUN == vb % per
        key = jnp.where(held, row * RUN + lanes(row.shape) % RUN, RUN * GROUP).astype(F32)
        on_own = rows_of((RUN, LANES)) == jnp.where(held, lanes(row.shape) % RUN, -1)
        key_down = jnp.sum(jnp.where(on_own, key, 0.0), axis=1, keepdims=True)
        label_down = jnp.sum(jnp.where(on_own, row.astype(F32), 0.0), axis=1, keepdims=True)
        place = jnp.sum(jnp.where(key < key_down, 1.0, 0.0), axis=1, keepdims=True)
        place_ref[part * RUN : (part + 1) * RUN, :] = jnp.broadcast_to(place, (RUN, LANES)).astype(I32)
        label_ref[part * RUN : (part + 1) * RUN, :] = jnp.broadcast_to(label_down, (RUN, label_ref.shape[1])).astype(I32)


def folded(part, span):
    count = part.shape[0]
    if span > count:
        return jnp.concatenate([part, jnp.zeros((span - count, part.shape[1]), F32)], 0)
    slots = span - 1
    row = rows_of((span, part.shape[1]))
    total = jnp.where(row < slots, part[:span], 0.0)
    for low in range(slots, count, slots):
        moved = pltpu.roll(part, count - low, 0)[:span]
        total = total + jnp.where(row < min(slots, count - low), moved, 0.0)
    return total


def multiply_kernel(span, move_ref, tag_ref, columns_ref, own_ref, other_ref, amp_ref, partner_ref, out_ref, sorted_ref):
    windows = own_ref.shape[0]
    per = LANES // RUN
    halves = amp_ref.shape[0] // LANES
    share = lax.axis_index("xl")
    for r in range(windows // per):
        block = jnp.concatenate([x for w in range(r * per, (r + 1) * per) for x in (own_ref[w], other_ref[w])], 0)
        sorted_ref[r * LANES : (r + 1) * LANES, :] = jnp.dot(
            move_ref[r], block, preferred_element_type=F32
        ).astype(BF16)
    for side, columns_of in enumerate((amp_ref, partner_ref)):
        first = (share if side == 0 else 1 - share) * windows
        for r in range(windows // per):
            at = slice(r * LANES, (r + 1) * LANES)
            sums = lax.dot_general(
                sorted_ref[at, :], columns_of[...], (((1,), (1,)), ((), ())), preferred_element_type=F32
            )
            tags = jnp.concatenate([tag_ref[at, :]] * halves, 1)
            sums = jnp.where(tags == columns_ref[8 * side : 8 * side + 1, :], sums, 0.0)
            for w in range(per):
                total = folded(sums[w * RUN : (w + 1) * RUN], span)
                largest = jnp.max(jnp.max(jnp.abs(total), axis=0, keepdims=True), axis=1, keepdims=True)
                power = jnp.ceil(jnp.log2(jnp.maximum(largest, SMALLEST)))
                total = total * jnp.exp2(TOP - power)
                code = total * jnp.abs(total)
                square = total * total
                for _ in range(ROOTS - 1):
                    code, square = code * square, square * square
                code = jnp.where(rows_of(code.shape) == span - 1, power, code).astype(BF16)
                for half in range(halves):
                    out_ref[first + r * per + w, half * span : (half + 1) * span, :] = code[:, half * LANES : (half + 1) * LANES]


def finish_kernel(span, columns_ref, place_ref, label_ref, parts_ref, out_ref):
    halves = out_ref.shape[1] // LANES
    sources = parts_ref.shape[0] // 2
    slots = span - 1
    for part in range(2):
        totals = []
        for half in range(halves):
            total = jnp.zeros((span, LANES), F32)
            for source in range(sources):
                code = parts_ref[part * sources + source, half * span : (half + 1) * span, :].astype(F32)
                root = jnp.abs(code)
                for _ in range(ROOTS):
                    root = jnp.sqrt(root)
                total = total + jnp.where(code < 0.0, -root, root) * jnp.exp2(code[span - 1 :, :] - TOP)
            totals.append(total)
        at = slice(part * RUN, (part + 1) * RUN)
        place = place_ref[at, 0:1]
        slot = jnp.where(place >= 2 * slots, place - 2 * slots, jnp.where(place >= slots, place - slots, place))
        chosen = jnp.where(lanes((RUN, span)) == slot, 1.0, 0.0).astype(BF16)
        full = jnp.dot(chosen, jnp.concatenate(totals, 1).astype(BF16), preferred_element_type=F32)
        full = jnp.where(label_ref[at, :] == columns_ref[0:1, :], full, 0.0).astype(BF16)
        half_run = RUN // 2
        for core in range(2):
            low = core * RUN + part * half_run
            out_ref[low : low + half_run, :] = full[core * half_run : (core + 1) * half_run]


def per_device(sizes, amplitudes, integrals, irrep_virt, irrep_occ, irrep_slab):
    va_axes = [(name, sizes[name]) for name in ("xl", "y", "c")]
    vb_axes = [(name, sizes[name]) for name in ("xh", "z")]
    a_rows, slab_count, width = amplitudes.shape
    b_rows = integrals.shape[0]
    depth = width // GROUP
    chips = sizes["xl"] * sizes["y"]
    columns = a_rows * slab_count
    shaped = jax.ShapeDtypeStruct
    share = b_rows // sizes["xl"]

    arrays = (irrep_virt, irrep_occ, irrep_slab, integrals, amplitudes.reshape(columns, width))
    small, amp_near, pair_tag, left_tag = pl.pallas_call(
        functools.partial(squeeze_int_kernel, va_axes, vb_axes),
        out_shape=(
            shaped((chips, share, depth), BF16),
            shaped((columns, width), BF16),
            shaped((width // LANES, LANES), I32),
            shaped((columns, LANES), I32),
        ),
        in_specs=[HBM] * 5,
        out_specs=(ANY, VMEM, VMEM, VMEM),
        scratch_shapes=[
            pltpu.SMEM(irrep_virt.shape, I32),
            pltpu.SMEM(irrep_occ.shape, I32),
            pltpu.SMEM(irrep_slab.shape, I32),
            pltpu.VMEM((b_rows, width), BF16),
            pltpu.VMEM((b_rows, depth), BF16),
            pltpu.SemaphoreType.DMA((4 + width // (GROUP * LANES) + chips,)),
        ],
        compiler_params=params(),
        name="squeeze_int",
    )(*(pltpu.with_memory_space_constraint(x, pltpu.HBM) for x in arrays))
    own = lax.all_to_all(small, ("xl", "y"), 0, 0, tiled=False)

    amp_small = pl.pallas_call(
        squeeze_amp_kernel,
        out_shape=shaped((columns, depth), BF16),
        in_specs=[VMEM] * 3,
        out_specs=VMEM,
        compiler_params=params(),
        cost_estimate=pl.CostEstimate(flops=4 << 30, transcendentals=0, bytes_accessed=8 << 20),
        name="squeeze_amp",
    )(pair_tag, left_tag, amp_near)
    amp_partner = lax.ppermute(amp_small, "xl", [(0, 1), (1, 0)])

    labels = irrep_virt.reshape(chips, sizes["c"], sizes["xl"], share).transpose(2, 0, 1, 3).reshape(-1, LANES)
    *plan, most = pl.pallas_call(
        functools.partial(plan_kernel, a_rows, va_axes, vb_axes),
        out_shape=(
            shaped((labels.shape[0] // 2, LANES, LANES), BF16),
            shaped((labels.size // 2, LANES), I32),
            shaped((16, columns), I32),
            shaped((WINDOW, LANES), I32),
            shaped((WINDOW, columns), I32),
            shaped((1,), I32),
        ),
        in_specs=[SMEM, SMEM, SMEM, VMEM],
        out_specs=(VMEM,) * 5 + (SMEM,),
        compiler_params=params(),
        cost_estimate=pl.CostEstimate(flops=2 << 30, transcendentals=0, bytes_accessed=4 << 20),
        name="plan",
    )(irrep_virt, irrep_occ, irrep_slab, labels)

    def rest(span, move, tags, column_labels, place, row_labels, own, other, amp_small, amp_partner):
        parts = pl.pallas_call(
            functools.partial(multiply_kernel, span),
            out_shape=shaped((2 * chips, columns // LANES * span, LANES), BF16),
            in_specs=[VMEM] * 7,
            out_specs=VMEM,
            scratch_shapes=[pltpu.VMEM((chips * RUN, depth), BF16)],
            compiler_params=params(),
            name="multiply",
        )(move, tags, column_labels, own, other, amp_small, amp_partner)
        parts = lax.all_to_all(parts, ("xl", "xh", "z"), 0, 0, tiled=False)
        return pl.pallas_call(
            functools.partial(finish_kernel, span),
            out_shape=shaped((WINDOW, columns), BF16),
            in_specs=[VMEM] * 4,
            out_specs=VMEM,
            compiler_params=params(),
            name="finish",
        )(column_labels, place, row_labels, parts)

    own, amp_small, most, *plan = lax.optimization_barrier((own, amp_small, most, *plan))
    other = lax.ppermute(own, "c", [(0, 1), (1, 0)])

    return lax.cond(
        most[0] < SPAN,
        functools.partial(rest, SPAN),
        functools.partial(rest, RUN + 8),
        *plan, own, other, amp_small, amp_partner,
    )


def solution(mesh):
    names = ("xl", "y", "c", "xh", "z")
    shape = (2, mesh.shape["va"] // 4, 2, 2, mesh.shape["vb"] // 2)
    fine = Mesh(mesh.devices.reshape(shape), names)
    va, vb = names[:3], names[3:]
    return jax.shard_map(
        functools.partial(per_device, dict(zip(names, shape))),
        mesh=fine,
        in_specs=(P(va, None, vb), P(va, vb), P(), P(), P()),
        out_specs=P(vb, va),
        check_vma=False,
    )
```

time: 56.2 us -> 53.1 us (0.945)
  waiting for transfers between devices: 10.5 us -> 4.73 us
  starting transfers between devices: 11.1 us -> 14.5 us
  blocking collectives: 23.4 us -> 25.4 us
  local copies, waits for them, and re-layouts: 2.61 us -> 0.84 us
  Pallas kernels: 7.45 us -> 6.57 us
    all_to_all x1, waiting for transfers between devices: 9.3 us -> 3.88 us  [per_device(): own = lax.all_to_all(small, ('xl', 'y'), 0, 0, tiled=False)]
    ppermute x0 -> x1, starting transfers between devices: none -> 3.42 us  [per_device(): amp_partner = lax.ppermute(amp_small, 'xl', [(0, 1), (1, 0)])]
    all_to_all x1, blocking collectives: 23.4 us -> 25.4 us  [rest(): parts = lax.all_to_all(parts, ('xl', 'xh', 'z'), 0, 0, tiled=False)]
    unnamed x10 -> x8, local copies, waits for them, and re-layouts: 2.61 us -> 0.63 us
    pallas_call x4, Pallas kernels: 4.95 us -> 4.12 us  [the longest x1 1.43 us: per_device(): pl.pallas_call(functools.partial(plan_kernel, a_rows, va_axes, vb_axes),...]
  transfers between devices with their start and end apart: 2 -> 3, of which waited for: 2 -> 2; matrix products, arithmetic and copies ran while one was open for 0% -> 0% of each run, Pallas kernels for 6% -> 4%
where the time goes in v3:
time: 53.1 us; the launch traced here: 52.8 us
  blocking collectives  25.4 us (48%)
  starting transfers between devices  14.5 us (27%)
  Pallas kernels  6.57 us (12%)
  waiting for transfers between devices  4.73 us (9%)
  local copies, waits for them, and re-layouts  0.84 us (2%)
  between operations  0.75 us (1%)
    all_to_all x1, blocking collectives, rest(): parts = lax.all_to_all(parts, ('xl', 'xh', 'z'), 0, 0, tiled=False)  25.4 us
    all_to_all x1, starting transfers between devices, per_device(): own = lax.all_to_all(small, ('xl', 'y'), 0, 0, tiled=False)  9.15 us
    all_to_all x1, waiting for transfers between devices, per_device(): own = lax.all_to_all(small, ('xl', 'y'), 0, 0, tiled=False)  3.88 us
    ppermute x1, starting transfers between devices, per_device(): amp_partner = lax.ppermute(amp_small, 'xl', [(0, 1), (1, 0)])  3.42 us
    pallas_call x1, Pallas kernels, per_device(): pl.pallas_call(functools.partial(squeeze_int_kernel, va_axes, vb_axes), o...  2.45 us
    ppermute x1, starting transfers between devices, per_device(): other = lax.ppermute(own, 'c', [(0, 1), (1, 0)])  1.91 us
    pallas_call x1, Pallas kernels, per_device(): pl.pallas_call(functools.partial(plan_kernel, a_rows, va_axes, vb_axes),...  1.43 us
    pallas_call x1, Pallas kernels, rest(): pl.pallas_call(functools.partial(multiply_kernel, span), out_shape=shaped...  1.2 us
  transfers between devices with their start and end apart: 3, of which 2 were waited for; matrix products, arithmetic and copies ran while one was open for 0% of the time, Pallas kernels for 4%

profile of v3, /device:TPU:8, one launch (start us, length us, event | category | flops | bytes accessed | tf_op | source)
XLA Modules:
  0.0 52.8 jit_solution(15307562551457214679)
XLA Ops:
  0.0 2.4 %squeeze_int.1 = (bf16[16,16,512]{2,1,0:T(8,128)(2,1)}, bf16[256,4096]{1,0:T(8,128)(2,1)S(1)}, s32[32,128]{1,0:T(8,128)S(1)}, s32[256,128]{1,0:T(8,128)S(1)}) custom-call(s32[1024]{0:T(1024)} %virt_ref.1, s32[64]{0:T(128)} %occ_ref.1, s32[8]{0:T(128)} %slab_ref.1, bf16[32,4096]{1,0:T(8,128)(2,1)} %int_hbm.1, bf16[256,4096]{1,0:T(8,128)(2,1)} %bitcast.3), custom_call_target="tpu_custom_call" | custom-call | tf_op jit(solution)/shard_map/squeeze_int/pallas_call | solution.py:291
  2.5 9.2 %all-to-all-start.2 = ((bf16[16,16,512]{2,1,0:T(8,128)(2,1)}), bf16[16,16,512]{2,1,0:T(8,128)(2,1)S(1)}, u32[]{:S(2)}, u32[]{:S(2)}) async-start(bf16[16,16,512]{2,1,0:T(8,128)(2,1)} %get-tuple-element.80), calls=%async_computation.2 | async-start | bytes 524288 | tf_op jit(solution)/shard_map/all_to_all | solution.py:312
  11.6 0.0 copy-start
  11.6 0.0 copy-start.1
  11.6 0.0 copy-start.2
  11.6 0.7 %squeeze_amp.1 = bf16[256,512]{1,0:T(8,128)(2,1)S(1)} custom-call(s32[32,128]{1,0:T(8,128)S(1)} %get-tuple-element.81.pair_ref, s32[256,128]{1,0:T(8,128)S(1)} %get-tuple-element.82.left_ref, bf16[256,4096]{1,0:T(8,128)(2,1)S(1)} %get-tuple-element.83.amp_ref), custom_call_target="tpu_custom_call" | custom-call | flops 4294967296 | bytes 8388608 | tf_op jit(solution)/shard_map/squeeze_amp/pallas_call | solution.py:314
  12.4 3.4 %collective-permute-start.1 = (bf16[256,512]{1,0:T(8,128)(2,1)S(1)}, bf16[256,512]{1,0:T(8,128)(2,1)S(1)}, u32[]{:S(2)}, u32[]{:S(2)}) collective-permute-start(bf16[256,512]{1,0:T(8,128)(2,1)S(1)} %squeeze_amp.1), channel_id=1, source_target_pairs={{0,256},{256,0},{1,257},{257,1},{2,258},{258,2},{3,259},{259,3},{4... | collective-permute-start | bytes 786440 | tf_op jit(solution)/shard_map/ppermute | solution.py:323
  15.8 0.0 copy-done
  15.8 0.1 reshape.14
  15.9 0.1 reshape.15.labels_ref
  16.0 0.0 copy-done.1
  16.0 0.0 copy-done.2
  16.1 1.4 %plan.1 = (bf16[4,128,128]{2,1,0:T(8,128)(2,1)S(1)}, s32[512,128]{1,0:T(8,128)S(1)}, s32[16,256]{1,0:T(8,128)S(1)}, s32[64,128]{1,0:T(8,128)S(1)}, s32[64,256]{1,0:T(8,128)S(1)}, /*index=5*/s32[1]{0:T(128)}) custom-call(s32[1024]{0:T(1024)S(1)} %copy-done, s32[64]{0:T(128)S(1)} %copy-done.1, s32[8]{0:T(128)S(1)} %copy-done.2, s32[8,128]{1,0:T(8,128)S(1)} %reshape.15.labels_ref), custom_call_target="tpu_custom_call" | custom-call | flops 2147483648 | bytes 4194304 | tf_op jit(solution)/shard_map/plan/pallas_call | solution.py:326
  17.5 3.9 %all-to-all-done.2 = bf16[16,16,512]{2,1,0:T(8,128)(2,1)S(1)} async-done(((bf16[16,16,512]{2,1,0:T(8,128)(2,1)}), bf16[16,16,512]{2,1,0:T(8,128)(2,1)S(1)}, u32[]{:S(2)}, u32[]{:S(2)}) %all-to-all-start.2) | async-done | bytes 262176 | tf_op jit(solution)/shard_map/all_to_all | solution.py:312
  21.4 1.9 %collective-permute-start = (bf16[16,16,512]{2,1,0:T(8,128)(2,1)S(1)}, bf16[16,16,512]{2,1,0:T(8,128)(2,1)S(1)}, u32[]{:S(2)}, u32[]{:S(2)}) collective-permute-start(bf16[16,16,512]{2,1,0:T(8,128)(2,1)S(1)} %all-to-all-done.2), channel_id=1, source_target_pairs={{0,16},{16,0},{1,17},{17,1},{2,18},{18,2},{3,19},{19,3},{4,20},{20... | collective-permute-start | bytes 786440 | tf_op jit(solution)/shard_map/ppermute | solution.py:364
  23.9 0.0 collective-permute-done.1
  24.0 0.8 %collective-permute-done = bf16[16,16,512]{2,1,0:T(8,128)(2,1)S(1)} collective-permute-done((bf16[16,16,512]{2,1,0:T(8,128)(2,1)S(1)}, bf16[16,16,512]{2,1,0:T(8,128)(2,1)S(1)}, u32[]{:S(2)}, u32[]{:S(2)}) %collective-permute-start) | collective-permute-done | bytes 262176 | tf_op jit(solution)/shard_map/ppermute | solution.py:364
  24.8 27.4 %conditional.1 = (bf16[64,256]{1,0:T(8,128)(2,1)S(1)}) conditional(s32[]{:T(128)} %bitcast.2, (bf16[4,128,128]{2,1,0:T(8,128)(2,1)S(1)}, s32[512,128]{1,0:T(8,128)S(1)}, s32[16,256]{1,0:T(8,128)S(1)}, bf16[16,16,512]{2,1,0:T(8,128)(2,1)S(1)}, bf16[16,16,512]{2,1,0:T(8,128)(2,1)S(1)}, /*index=5*/bf16[256,512]{1,0:T(8,128)(2,1)S(1)}, ...), branch_computations={%region_0.0_spmd, %region_1.0_spmd} | conditional | bytes 1310728 | solution.py:366
  24.8 1.2 %multiply.3 = bf16[32,32,128]{2,1,0:T(8,128)(2,1)S(1)} custom-call(bf16[4,128,128]{2,1,0:T(8,128)(2,1)S(1)} %get-tuple-element.56.move_ref, s32[512,128]{1,0:T(8,128)S(1)} %get-tuple-element.57.tag_ref, s32[16,256]{1,0:T(8,128)S(1)} %get-tuple-element.53.columns_ref, bf16[16,16,512]{2,1,0:T(8,128)(2,1)S(1)} %get-tuple-element.58.own_ref, ...), custom_call_target="tpu_custom_call" | custom-call | tf_op jit(solution)/shard_map/cond/branch_1_fun/multiply/pallas_call | solution.py:344
  26.0 25.4 %all_to_all.14.parts_ref = bf16[32,32,128]{2,1,0:T(8,128)(2,1)S(1)} all-to-all(bf16[32,32,128]{2,1,0:T(8,128)(2,1)S(1)} %multiply.3), channel_id=1, replica_groups=mesh['xl'=2,'y'=8,'c'=2,'xh'=2,'z'=8] {'xl','xh','z'}, dimensions={0} | all-to-all | bytes 524288 | tf_op jit(solution)/shard_map/cond/branch_1_fun/all_to_all | solution.py:353
  51.4 0.8 %finish.3 = bf16[64,256]{1,0:T(8,128)(2,1)S(1)} custom-call(s32[16,256]{1,0:T(8,128)S(1)} %get-tuple-element.53.columns_ref, s32[64,128]{1,0:T(8,128)S(1)} %get-tuple-element.54.place_ref, s32[64,256]{1,0:T(8,128)S(1)} %get-tuple-element.55.label_ref, bf16[32,32,128]{2,1,0:T(8,128)(2,1)S(1)} %all_to_all.14.parts_ref), custom_call_target="tpu_custom_call" | custom-call | tf_op jit(solution)/shard_map/cond/branch_1_fun/finish/pallas_call | solution.py:354
  52.2 0.0 copy-start.3
  52.2 0.6 %copy-done.3 = bf16[64,256]{1,0:T(8,128)(2,1)} copy-done((bf16[64,256]{1,0:T(8,128)(2,1)}, bf16[64,256]{1,0:T(8,128)(2,1)S(1)}, u32[]{:S(2)}) %copy-start.3) | copy-done | bytes 32792
  (1 shorter events, 0.0 us)
Async XLA Ops:
  2.5 18.9 %all-to-all-start.2 = ((bf16[16,16,512]{2,1,0:T(8,128)(2,1)}), bf16[16,16,512]{2,1,0:T(8,128)(2,1)S(1)}, u32[]{:S(2)}, u32[]{:S(2)}) async-start(bf16[16,16,512]{2,1,0:T(8,128)(2,1)} %get-tuple-element.80), calls=%async_computation.2 | async-start | bytes 524288 | tf_op jit(solution)/shard_map/all_to_all | solution.py:312
  11.6 4.2 %copy-start = (s32[1024]{0:T(1024)S(1)}, s32[1024]{0:T(1024)}, u32[]{:S(2)}) copy-start(s32[1024]{0:T(1024)} %virt_ref.1) | copy-start | bytes 12292
  11.6 4.4 %copy-start.1 = (s32[64]{0:T(128)S(1)}, s32[64]{0:T(128)}, u32[]{:S(2)}) copy-start(s32[64]{0:T(128)} %occ_ref.1) | copy-start | bytes 772
  11.6 4.4 %copy-start.2 = (s32[8]{0:T(128)S(1)}, s32[8]{0:T(128)}, u32[]{:S(2)}) copy-start(s32[8]{0:T(128)} %slab_ref.1) | copy-start | bytes 100
  12.4 11.6 %collective-permute-start.1 = (bf16[256,512]{1,0:T(8,128)(2,1)S(1)}, bf16[256,512]{1,0:T(8,128)(2,1)S(1)}, u32[]{:S(2)}, u32[]{:S(2)}) collective-permute-start(bf16[256,512]{1,0:T(8,128)(2,1)S(1)} %squeeze_amp.1), channel_id=1, source_target_pairs={{0,256},{256,0},{1,257},{257,1},{2,258},{258,2},{3,259},{259,3},{4... | collective-permute-start | bytes 786440 | tf_op jit(solution)/shard_map/ppermute | solution.py:323
  21.4 3.4 %collective-permute-start = (bf16[16,16,512]{2,1,0:T(8,128)(2,1)S(1)}, bf16[16,16,512]{2,1,0:T(8,128)(2,1)S(1)}, u32[]{:S(2)}, u32[]{:S(2)}) collective-permute-start(bf16[16,16,512]{2,1,0:T(8,128)(2,1)S(1)} %all-to-all-done.2), channel_id=1, source_target_pairs={{0,16},{16,0},{1,17},{17,1},{2,18},{18,2},{3,19},{19,3},{4,20},{20... | collective-permute-start | bytes 786440 | tf_op jit(solution)/shard_map/ppermute | solution.py:364
  52.2 0.6 %copy-start.3 = (bf16[64,256]{1,0:T(8,128)(2,1)}, bf16[64,256]{1,0:T(8,128)(2,1)S(1)}, u32[]{:S(2)}) copy-start(bf16[64,256]{1,0:T(8,128)(2,1)S(1)} %get-tuple-element.106) | copy-start | bytes 98308

commit v4 on v3

--- a/solution.py
+++ b/solution.py
@@ -14,7 +14,7 @@
 SMALLEST = 2.0**-100
 WINDOW = 64
 RUN = 32
-SPAN = 16
+SPANS = (12, 16)
 
 F32, BF16, I32 = jnp.float32, jnp.bfloat16, jnp.int32
 SMEM = pl.BlockSpec(memory_space=pltpu.SMEM)
@@ -92,6 +92,7 @@
         copy.wait()
     occ = occ_lanes(occ_ref)
     row_tag = spread(virt_ref, va * row_count, row_count, rows_of((row_count, LANES))) ^ occ_ref[0]
+    stacked = []
     for part in range(parts):
         fetch[3 + part].wait()
         kept = []
@@ -101,8 +102,10 @@
             pair_ref[at : at + 1, :] = tag
             held = int_ref[:, at * LANES : (at + 1) * LANES].astype(F32)
             kept.append(jnp.where(row_tag == tag, held, 0.0).astype(BF16))
-        small = jnp.dot(jnp.concatenate(kept, 1), squeeze, preferred_element_type=F32)
-        small_ref[:, part * LANES : (part + 1) * LANES] = small.astype(BF16)
+        stacked.append(jnp.concatenate(kept, 1))
+    small = jnp.dot(jnp.concatenate(stacked, 0), squeeze, preferred_element_type=F32).astype(BF16)
+    for part in range(parts):
+        small_ref[:, part * LANES : (part + 1) * LANES] = small[part * row_count : (part + 1) * row_count]
     peers, share = out_hbm.shape[0], out_hbm.shape[1]
     copies = []
     for peer in range(peers):
@@ -150,7 +153,7 @@
     a_count, va_axes, vb_axes, virt_ref, occ_ref, slab_ref, labels_ref,
     move_ref, tag_ref, columns_ref, place_ref, label_ref, most_ref,
 ):
-    core, share = lax.axis_index("c"), lax.axis_index("xl")
+    share = lax.axis_index("xl")
     va, vb = first_of(va_axes), first_of(vb_axes)
     across = va_axes[1][1] * va_axes[2][1]
     partner = va + (1 - 2 * share) * across
@@ -169,17 +172,8 @@
     count = labels.shape[0] // 2
     mine = jnp.where(share == 0, labels[:count], labels[count:])
     mine = jnp.concatenate([mine, mine], 0)
-    keys = sort_keys(mine)
-    keys_down = jnp.transpose(keys.astype(F32))
-    half = RUN // 2
-    swap = (lanes(keys.shape) // half) % 2 == 0
-
-    def own_first(x):
-        x = x.astype(F32)
-        swapped = jnp.where(swap, pltpu.roll(x, LANES - half, 1), pltpu.roll(x, half, 1))
-        return jnp.where(core == 0, x, swapped)
-
-    keys_across, labels_across = own_first(keys), own_first(mine)
+    keys_across, labels_across = sort_keys(mine).astype(F32), mine.astype(F32)
+    keys_down = jnp.transpose(keys_across)
     square = (LANES, LANES)
     for r in range(count):
         before = jnp.where(keys_down[:, r : r + 1] < keys_across[r : r + 1, :], 1.0, 0.0)
@@ -216,13 +210,13 @@
     return total
 
 
-def multiply_kernel(span, move_ref, tag_ref, columns_ref, own_ref, other_ref, amp_ref, partner_ref, out_ref, sorted_ref):
-    windows = own_ref.shape[0]
+def multiply_kernel(span, move_ref, tag_ref, columns_ref, rows_ref, amp_ref, partner_ref, out_ref, sorted_ref):
+    cores, windows = rows_ref.shape[:2]
     per = LANES // RUN
     halves = amp_ref.shape[0] // LANES
     share = lax.axis_index("xl")
     for r in range(windows // per):
-        block = jnp.concatenate([x for w in range(r * per, (r + 1) * per) for x in (own_ref[w], other_ref[w])], 0)
+        block = jnp.concatenate([x for w in range(r * per, (r + 1) * per) for x in [rows_ref[core, w] for core in range(cores)]], 0)
         sorted_ref[r * LANES : (r + 1) * LANES, :] = jnp.dot(
             move_ref[r], block, preferred_element_type=F32
         ).astype(BF16)
@@ -340,16 +334,16 @@
         name="plan",
     )(irrep_virt, irrep_occ, irrep_slab, labels)
 
-    def rest(span, move, tags, column_labels, place, row_labels, own, other, amp_small, amp_partner):
+    def rest(span, move, tags, column_labels, place, row_labels, both, amp_small, amp_partner):
         parts = pl.pallas_call(
             functools.partial(multiply_kernel, span),
             out_shape=shaped((2 * chips, columns // LANES * span, LANES), BF16),
-            in_specs=[VMEM] * 7,
+            in_specs=[VMEM] * 6,
             out_specs=VMEM,
             scratch_shapes=[pltpu.VMEM((chips * RUN, depth), BF16)],
             compiler_params=params(),
             name="multiply",
-        )(move, tags, column_labels, own, other, amp_small, amp_partner)
+        )(move, tags, column_labels, both, amp_small, amp_partner)
         parts = lax.all_to_all(parts, ("xl", "xh", "z"), 0, 0, tiled=False)
         return pl.pallas_call(
             functools.partial(finish_kernel, span),
@@ -361,13 +355,12 @@
         )(column_labels, place, row_labels, parts)
 
     own, amp_small, most, *plan = lax.optimization_barrier((own, amp_small, most, *plan))
-    other = lax.ppermute(own, "c", [(0, 1), (1, 0)])
-
-    return lax.cond(
-        most[0] < SPAN,
-        functools.partial(rest, SPAN),
-        functools.partial(rest, RUN + 8),
-        *plan, own, other, amp_small, amp_partner,
+    both = lax.all_gather(own, "c", axis=0, tiled=False)
+
+    return lax.switch(
+        sum((most[0] >= span).astype(I32) for span in SPANS),
+        [functools.partial(rest, span) for span in (*SPANS, RUN + 8)],
+        *plan, both, amp_small, amp_partner,
     )
 
 

time: 53.1 us -> 51.8 us (0.976)
  starting transfers between devices: 14.5 us -> 12.6 us
  blocking collectives: 25.4 us -> 26.5 us
  waiting for transfers between devices: 4.73 us -> 3.86 us
  between operations: 0.75 us -> 1.39 us
    all_gather x0 -> x1, blocking collectives: none -> 2.18 us  [per_device(): both = lax.all_gather(own, 'c', axis=0, tiled=False)]
    ppermute x1 -> x0, starting transfers between devices: 1.91 us -> none  [per_device(): other = lax.ppermute(own, 'c', [(0, 1), (1, 0)])]
    all_to_all x1, blocking collectives: 25.4 us -> 24.3 us  [rest(): parts = lax.all_to_all(parts, ('xl', 'xh', 'z'), 0, 0, tiled=False)]
    ppermute x1 -> x0, waiting for transfers between devices: 0.84 us -> none  [per_device(): other = lax.ppermute(own, 'c', [(0, 1), (1, 0)])]
  transfers between devices with their start and end apart: 3 -> 2, of which waited for: 2 -> 1; matrix products, arithmetic and copies ran while one was open for 0% -> 0% of each run, Pallas kernels for 4% -> 4%
where the time goes in v4:
time: 51.8 us; the launch traced here: 51.5 us
  blocking collectives  26.5 us (51%)
  starting transfers between devices  12.6 us (24%)
  Pallas kernels  6.32 us (12%)
  waiting for transfers between devices  3.86 us (7%)
  between operations  1.39 us (3%)
  local copies, waits for them, and re-layouts  0.84 us (2%)
    all_to_all x1, blocking collectives, rest(): parts = lax.all_to_all(parts, ('xl', 'xh', 'z'), 0, 0, tiled=False)  24.3 us
    all_to_all x1, starting transfers between devices, per_device(): own = lax.all_to_all(small, ('xl', 'y'), 0, 0, tiled=False)  9.16 us
    all_to_all x1, waiting for transfers between devices, per_device(): own = lax.all_to_all(small, ('xl', 'y'), 0, 0, tiled=False)  3.86 us
    ppermute x1, starting transfers between devices, per_device(): amp_partner = lax.ppermute(amp_small, 'xl', [(0, 1), (1, 0)])  3.43 us
    all_gather x1, blocking collectives, per_device(): both = lax.all_gather(own, 'c', axis=0, tiled=False)  2.18 us
    pallas_call x1, Pallas kernels, per_device(): pl.pallas_call(functools.partial(squeeze_int_kernel, va_axes, vb_axes), o...  2.09 us
    pallas_call x1, Pallas kernels, per_device(): pl.pallas_call(functools.partial(plan_kernel, a_rows, va_axes, vb_axes),...  1.45 us
    pallas_call x1, Pallas kernels, rest(): pl.pallas_call(functools.partial(multiply_kernel, span), out_shape=shaped...  1.29 us
  transfers between devices with their start and end apart: 2, of which 1 were waited for; matrix products, arithmetic and copies ran while one was open for 0% of the time, Pallas kernels for 4%

profile of v4, /device:TPU:8, one launch (start us, length us, event | category | flops | bytes accessed | tf_op | source)
XLA Modules:
  0.0 51.5 jit_solution(6391632464146897156)
XLA Ops:
  0.0 2.1 %squeeze_int.1 = (bf16[16,16,512]{2,1,0:T(8,128)(2,1)}, bf16[256,4096]{1,0:T(8,128)(2,1)S(1)}, s32[32,128]{1,0:T(8,128)S(1)}, s32[256,128]{1,0:T(8,128)S(1)}) custom-call(s32[1024]{0:T(1024)} %virt_ref.1, s32[64]{0:T(128)} %occ_ref.1, s32[8]{0:T(128)} %slab_ref.1, bf16[32,4096]{1,0:T(8,128)(2,1)} %int_hbm.1, bf16[256,4096]{1,0:T(8,128)(2,1)} %bitcast.7), custom_call_target="tpu_custom_call" | custom-call | tf_op jit(solution)/shard_map/squeeze_int/pallas_call | solution.py:285
  2.1 9.2 %all-to-all-start.3 = ((bf16[16,16,512]{2,1,0:T(8,128)(2,1)}), bf16[16,16,512]{2,1,0:T(8,128)(2,1)S(1)}, u32[]{:S(2)}, u32[]{:S(2)}) async-start(bf16[16,16,512]{2,1,0:T(8,128)(2,1)} %get-tuple-element.99), calls=%async_computation.3 | async-start | bytes 524288 | tf_op jit(solution)/shard_map/all_to_all | solution.py:306
  11.3 0.0 copy-start
  11.3 0.0 copy-start.1
  11.3 0.0 copy-start.2
  11.3 0.7 %squeeze_amp.1 = bf16[256,512]{1,0:T(8,128)(2,1)S(1)} custom-call(s32[32,128]{1,0:T(8,128)S(1)} %get-tuple-element.100.pair_ref, s32[256,128]{1,0:T(8,128)S(1)} %get-tuple-element.101.left_ref, bf16[256,4096]{1,0:T(8,128)(2,1)S(1)} %get-tuple-element.102.amp_ref), custom_call_target="tpu_custom_call" | custom-call | flops 4294967296 | bytes 8388608 | tf_op jit(solution)/shard_map/squeeze_amp/pallas_call | solution.py:308
  12.0 3.4 %collective-permute-start = (bf16[256,512]{1,0:T(8,128)(2,1)S(1)}, bf16[256,512]{1,0:T(8,128)(2,1)S(1)}, u32[]{:S(2)}, u32[]{:S(2)}) collective-permute-start(bf16[256,512]{1,0:T(8,128)(2,1)S(1)} %squeeze_amp.1), channel_id=1, source_target_pairs={{0,256},{256,0},{1,257},{257,1},{2,258},{258,2},{3,259},{259,3},{4... | collective-permute-start | bytes 786440 | tf_op jit(solution)/shard_map/ppermute | solution.py:317
  15.5 0.0 copy-done
  15.5 0.1 reshape.20
  15.6 0.1 reshape.21.labels_ref
  15.7 0.0 copy-done.1
  15.7 0.0 copy-done.2
  15.7 1.4 %plan.1 = (bf16[4,128,128]{2,1,0:T(8,128)(2,1)S(1)}, s32[512,128]{1,0:T(8,128)S(1)}, s32[16,256]{1,0:T(8,128)S(1)}, s32[64,128]{1,0:T(8,128)S(1)}, s32[64,256]{1,0:T(8,128)S(1)}, /*index=5*/s32[1]{0:T(128)}) custom-call(s32[1024]{0:T(1024)S(1)} %copy-done, s32[64]{0:T(128)S(1)} %copy-done.1, s32[8]{0:T(128)S(1)} %copy-done.2, s32[8,128]{1,0:T(8,128)S(1)} %reshape.21.labels_ref), custom_call_target="tpu_custom_call" | custom-call | flops 2147483648 | bytes 4194304 | tf_op jit(solution)/shard_map/plan/pallas_call | solution.py:320
  17.2 3.9 %all-to-all-done.3 = bf16[16,16,512]{2,1,0:T(8,128)(2,1)S(1)} async-done(((bf16[16,16,512]{2,1,0:T(8,128)(2,1)}), bf16[16,16,512]{2,1,0:T(8,128)(2,1)S(1)}, u32[]{:S(2)}, u32[]{:S(2)}) %all-to-all-start.3) | async-done | bytes 262176 | tf_op jit(solution)/shard_map/all_to_all | solution.py:306
  22.3 2.2 %all-gather = bf16[32,16,512]{2,1,0:T(8,128)(2,1)S(1)} all-gather(bf16[16,16,512]{2,1,0:T(8,128)(2,1)S(1)} %all-to-all-done.3), channel_id=2, replica_groups=mesh['xl'=2,'y'=8,'c'=2,'xh'=2,'z'=8] {'c'}, dimensions={0}, use_global_device_ids=true | all-gather | bytes 786432 | tf_op jit(solution)/shard_map/all_gather | solution.py:358
  24.5 0.0 collective-permute-done
  24.5 26.4 %conditional.1 = (bf16[64,256]{1,0:T(8,128)(2,1)S(1)}) conditional(s32[]{:T(128)} %bitcast.2, (bf16[4,128,128]{2,1,0:T(8,128)(2,1)S(1)}, s32[512,128]{1,0:T(8,128)S(1)}, s32[16,256]{1,0:T(8,128)S(1)}, bf16[2,16,16,512]{3,2,1,0:T(8,128)(2,1)S(1)}, bf16[256,512]{1,0:T(8,128)(2,1)S(1)}, /*index=5*/bf16[256,512]{1,0:T(8,128)(2,1)S(1)}, ...), branch_computations={%region_0.0_spmd, %region_1.0_spmd, %region_2.0_spmd} | conditional | bytes 1310728 | solution.py:360
  24.5 1.3 %multiply.3 = bf16[32,24,128]{2,1,0:T(8,128)(2,1)S(1)} custom-call(bf16[4,128,128]{2,1,0:T(8,128)(2,1)S(1)} %get-tuple-element.60.move_ref, s32[512,128]{1,0:T(8,128)S(1)} %get-tuple-element.61.tag_ref, s32[16,256]{1,0:T(8,128)S(1)} %get-tuple-element.56.columns_ref, bf16[2,16,16,512]{3,2,1,0:T(8,128)(2,1)S(1)} %get-tuple-element.62.rows_ref, ...), custom_call_target="tpu_custom_call" | custom-call | tf_op jit(solution)/shard_map/cond/branch_0_fun/multiply/pallas_call | solution.py:338
  25.8 24.3 %all_to_all.17.parts_ref = bf16[32,24,128]{2,1,0:T(8,128)(2,1)S(1)} all-to-all(bf16[32,24,128]{2,1,0:T(8,128)(2,1)S(1)} %multiply.3), channel_id=1, replica_groups=mesh['xl'=2,'y'=8,'c'=2,'xh'=2,'z'=8] {'xl','xh','z'}, dimensions={0} | all-to-all | bytes 393216 | tf_op jit(solution)/shard_map/cond/branch_0_fun/all_to_all | solution.py:347
  50.2 0.8 %finish.3 = bf16[64,256]{1,0:T(8,128)(2,1)S(1)} custom-call(s32[16,256]{1,0:T(8,128)S(1)} %get-tuple-element.56.columns_ref, s32[64,128]{1,0:T(8,128)S(1)} %get-tuple-element.58.place_ref, s32[64,256]{1,0:T(8,128)S(1)} %get-tuple-element.59.label_ref, bf16[32,24,128]{2,1,0:T(8,128)(2,1)S(1)} %all_to_all.17.parts_ref), custom_call_target="tpu_custom_call" | custom-call | tf_op jit(solution)/shard_map/cond/branch_0_fun/finish/pallas_call | solution.py:348
  50.9 0.0 copy-start.3
  50.9 0.6 %copy-done.3 = bf16[64,256]{1,0:T(8,128)(2,1)} copy-done((bf16[64,256]{1,0:T(8,128)(2,1)}, bf16[64,256]{1,0:T(8,128)(2,1)S(1)}, u32[]{:S(2)}) %copy-start.3) | copy-done | bytes 32792
  (1 shorter events, 0.0 us)
Async XLA Ops:
  2.1 18.9 %all-to-all-start.3 = ((bf16[16,16,512]{2,1,0:T(8,128)(2,1)}), bf16[16,16,512]{2,1,0:T(8,128)(2,1)S(1)}, u32[]{:S(2)}, u32[]{:S(2)}) async-start(bf16[16,16,512]{2,1,0:T(8,128)(2,1)} %get-tuple-element.99), calls=%async_computation.3 | async-start | bytes 524288 | tf_op jit(solution)/shard_map/all_to_all | solution.py:306
  11.3 4.2 %copy-start = (s32[1024]{0:T(1024)S(1)}, s32[1024]{0:T(1024)}, u32[]{:S(2)}) copy-start(s32[1024]{0:T(1024)} %virt_ref.1) | copy-start | bytes 12292
  11.3 4.4 %copy-start.1 = (s32[64]{0:T(128)S(1)}, s32[64]{0:T(128)}, u32[]{:S(2)}) copy-start(s32[64]{0:T(128)} %occ_ref.1) | copy-start | bytes 772
  11.3 4.4 %copy-start.2 = (s32[8]{0:T(128)S(1)}, s32[8]{0:T(128)}, u32[]{:S(2)}) copy-start(s32[8]{0:T(128)} %slab_ref.1) | copy-start | bytes 100
  12.0 12.5 %collective-permute-start = (bf16[256,512]{1,0:T(8,128)(2,1)S(1)}, bf16[256,512]{1,0:T(8,128)(2,1)S(1)}, u32[]{:S(2)}, u32[]{:S(2)}) collective-permute-start(bf16[256,512]{1,0:T(8,128)(2,1)S(1)} %squeeze_amp.1), channel_id=1, source_target_pairs={{0,256},{256,0},{1,257},{257,1},{2,258},{258,2},{3,259},{259,3},{4... | collective-permute-start | bytes 786440 | tf_op jit(solution)/shard_map/ppermute | solution.py:317
  50.9 0.6 %copy-start.3 = (bf16[64,256]{1,0:T(8,128)(2,1)}, bf16[64,256]{1,0:T(8,128)(2,1)S(1)}, u32[]{:S(2)}) copy-start(bf16[64,256]{1,0:T(8,128)(2,1)S(1)} %get-tuple-element.124) | copy-start | bytes 98308

commit v5 on v4

--- a/solution.py
+++ b/solution.py
@@ -253,9 +253,7 @@
             total = jnp.zeros((span, LANES), F32)
             for source in range(sources):
                 code = parts_ref[part * sources + source, half * span : (half + 1) * span, :].astype(F32)
-                root = jnp.abs(code)
-                for _ in range(ROOTS):
-                    root = jnp.sqrt(root)
+                root = jnp.exp2(jnp.log2(jnp.abs(code)) * 0.5**ROOTS)
                 total = total + jnp.where(code < 0.0, -root, root) * jnp.exp2(code[span - 1 :, :] - TOP)
             totals.append(total)
         at = slice(part * RUN, (part + 1) * RUN)
@@ -354,11 +352,12 @@
             name="finish",
         )(column_labels, place, row_labels, parts)
 
-    own, amp_small, most, *plan = lax.optimization_barrier((own, amp_small, most, *plan))
+    tier = sum((most[0] >= span).astype(I32) for span in SPANS)
+    own, amp_small, tier, *plan = lax.optimization_barrier((own, amp_small, tier, *plan))
     both = lax.all_gather(own, "c", axis=0, tiled=False)
 
     return lax.switch(
-        sum((most[0] >= span).astype(I32) for span in SPANS),
+        tier,
         [functools.partial(rest, span) for span in (*SPANS, RUN + 8)],
         *plan, both, amp_small, amp_partner,
     )

time: 51.8 us -> 50.1 us (0.967)
  waiting for transfers between devices: 3.86 us -> 2.57 us
    all_to_all x1, waiting for transfers between devices: 3.86 us -> 2.56 us  [per_device(): own = lax.all_to_all(small, ('xl', 'y'), 0, 0, tiled=False)]
where the time goes in v5:
time: 50.1 us; the launch traced here: 49.8 us
  blocking collectives  26.5 us (53%)
  starting transfers between devices  12.6 us (25%)
  Pallas kernels  5.88 us (12%)
  waiting for transfers between devices  2.57 us (5%)
  between operations  1.39 us (3%)
  local copies, waits for them, and re-layouts  0.84 us (2%)
    all_to_all x1, blocking collectives, rest(): parts = lax.all_to_all(parts, ('xl', 'xh', 'z'), 0, 0, tiled=False)  24.3 us
    all_to_all x1, starting transfers between devices, per_device(): own = lax.all_to_all(small, ('xl', 'y'), 0, 0, tiled=False)  9.16 us
    ppermute x1, starting transfers between devices, per_device(): amp_partner = lax.ppermute(amp_small, 'xl', [(0, 1), (1, 0)])  3.43 us
    all_to_all x1, waiting for transfers between devices, per_device(): own = lax.all_to_all(small, ('xl', 'y'), 0, 0, tiled=False)  2.56 us
    all_gather x1, blocking collectives, per_device(): both = lax.all_gather(own, 'c', axis=0, tiled=False)  2.17 us
    pallas_call x1, Pallas kernels, per_device(): pl.pallas_call(functools.partial(squeeze_int_kernel, va_axes, vb_axes), o...  2.09 us
    pallas_call x1, Pallas kernels, per_device(): pl.pallas_call(functools.partial(plan_kernel, a_rows, va_axes, vb_axes),...  1.45 us
    pallas_call x1, Pallas kernels, rest(): pl.pallas_call(functools.partial(multiply_kernel, span), out_shape=shaped...  1.29 us
  transfers between devices with their start and end apart: 2, of which 1 were waited for; matrix products, arithmetic and copies ran while one was open for 0% of the time, Pallas kernels for 4%

profile of v5, /device:TPU:8, one launch (start us, length us, event | category | flops | bytes accessed | tf_op | source)
XLA Modules:
  0.0 49.8 jit_solution(9077749555102670121)
XLA Ops:
  0.0 2.1 %squeeze_int.1 = (bf16[16,16,512]{2,1,0:T(8,128)(2,1)}, bf16[256,4096]{1,0:T(8,128)(2,1)S(1)}, s32[32,128]{1,0:T(8,128)S(1)}, s32[256,128]{1,0:T(8,128)S(1)}) custom-call(s32[1024]{0:T(1024)} %virt_ref.1, s32[64]{0:T(128)} %occ_ref.1, s32[8]{0:T(128)} %slab_ref.1, bf16[32,4096]{1,0:T(8,128)(2,1)} %int_hbm.1, bf16[256,4096]{1,0:T(8,128)(2,1)} %bitcast.7), custom_call_target="tpu_custom_call" | custom-call | tf_op jit(solution)/shard_map/squeeze_int/pallas_call | solution.py:283
  2.1 9.2 %all-to-all-start.3 = ((bf16[16,16,512]{2,1,0:T(8,128)(2,1)}), bf16[16,16,512]{2,1,0:T(8,128)(2,1)S(1)}, u32[]{:S(2)}, u32[]{:S(2)}) async-start(bf16[16,16,512]{2,1,0:T(8,128)(2,1)} %get-tuple-element.99), calls=%async_computation.3 | async-start | bytes 524288 | tf_op jit(solution)/shard_map/all_to_all | solution.py:304
  11.3 0.0 copy-start
  11.3 0.0 copy-start.1
  11.3 0.0 copy-start.2
  11.3 0.7 %squeeze_amp.1 = bf16[256,512]{1,0:T(8,128)(2,1)S(1)} custom-call(s32[32,128]{1,0:T(8,128)S(1)} %get-tuple-element.100.pair_ref, s32[256,128]{1,0:T(8,128)S(1)} %get-tuple-element.101.left_ref, bf16[256,4096]{1,0:T(8,128)(2,1)S(1)} %get-tuple-element.102.amp_ref), custom_call_target="tpu_custom_call" | custom-call | flops 4294967296 | bytes 8388608 | tf_op jit(solution)/shard_map/squeeze_amp/pallas_call | solution.py:306
  12.0 3.4 %collective-permute-start = (bf16[256,512]{1,0:T(8,128)(2,1)S(1)}, bf16[256,512]{1,0:T(8,128)(2,1)S(1)}, u32[]{:S(2)}, u32[]{:S(2)}) collective-permute-start(bf16[256,512]{1,0:T(8,128)(2,1)S(1)} %squeeze_amp.1), channel_id=1, source_target_pairs={{0,256},{256,0},{1,257},{257,1},{2,258},{258,2},{3,259},{259,3},{4... | collective-permute-start | bytes 786440 | tf_op jit(solution)/shard_map/ppermute | solution.py:315
  15.5 0.0 copy-done
  15.5 0.1 reshape.17
  15.6 0.1 reshape.18.labels_ref
  15.7 0.0 copy-done.1
  15.7 0.0 copy-done.2
  15.7 1.4 %plan.1 = (bf16[4,128,128]{2,1,0:T(8,128)(2,1)S(1)}, s32[512,128]{1,0:T(8,128)S(1)}, s32[16,256]{1,0:T(8,128)S(1)}, s32[64,128]{1,0:T(8,128)S(1)}, s32[64,256]{1,0:T(8,128)S(1)}, /*index=5*/s32[1]{0:T(128)}) custom-call(s32[1024]{0:T(1024)S(1)} %copy-done, s32[64]{0:T(128)S(1)} %copy-done.1, s32[8]{0:T(128)S(1)} %copy-done.2, s32[8,128]{1,0:T(8,128)S(1)} %reshape.18.labels_ref), custom_call_target="tpu_custom_call" | custom-call | flops 2147483648 | bytes 4194304 | tf_op jit(solution)/shard_map/plan/pallas_call | solution.py:318
  18.5 2.6 %all-to-all-done.3 = bf16[16,16,512]{2,1,0:T(8,128)(2,1)S(1)} async-done(((bf16[16,16,512]{2,1,0:T(8,128)(2,1)}), bf16[16,16,512]{2,1,0:T(8,128)(2,1)S(1)}, u32[]{:S(2)}, u32[]{:S(2)}) %all-to-all-start.3) | async-done | bytes 262176 | tf_op jit(solution)/shard_map/all_to_all | solution.py:304
  21.0 2.2 %all-gather = bf16[32,16,512]{2,1,0:T(8,128)(2,1)S(1)} all-gather(bf16[16,16,512]{2,1,0:T(8,128)(2,1)S(1)} %all-to-all-done.3), channel_id=2, replica_groups=mesh['xl'=2,'y'=8,'c'=2,'xh'=2,'z'=8] {'c'}, dimensions={0}, use_global_device_ids=true | all-gather | bytes 786432 | tf_op jit(solution)/shard_map/all_gather | solution.py:357
  23.2 0.0 collective-permute-done
  23.2 26.0 %conditional.1 = (bf16[64,256]{1,0:T(8,128)(2,1)S(1)}) conditional(s32[]{:T(128)} %clamp.3, (bf16[4,128,128]{2,1,0:T(8,128)(2,1)S(1)}, s32[512,128]{1,0:T(8,128)S(1)}, s32[16,256]{1,0:T(8,128)S(1)}, bf16[2,16,16,512]{3,2,1,0:T(8,128)(2,1)S(1)}, bf16[256,512]{1,0:T(8,128)(2,1)S(1)}, /*index=5*/bf16[256,512]{1,0:T(8,128)(2,1)S(1)}, ...), branch_computations={%region_0.0_spmd, %region_1.0_spmd, %region_2.0_spmd} | conditional | bytes 1310728 | solution.py:359
  23.2 1.3 %multiply.3 = bf16[32,24,128]{2,1,0:T(8,128)(2,1)S(1)} custom-call(bf16[4,128,128]{2,1,0:T(8,128)(2,1)S(1)} %get-tuple-element.60.move_ref, s32[512,128]{1,0:T(8,128)S(1)} %get-tuple-element.61.tag_ref, s32[16,256]{1,0:T(8,128)S(1)} %get-tuple-element.56.columns_ref, bf16[2,16,16,512]{3,2,1,0:T(8,128)(2,1)S(1)} %get-tuple-element.62.rows_ref, ...), custom_call_target="tpu_custom_call" | custom-call | tf_op jit(solution)/shard_map/cond/branch_0_fun/multiply/pallas_call | solution.py:336
  24.5 24.3 %all_to_all.17.parts_ref = bf16[32,24,128]{2,1,0:T(8,128)(2,1)S(1)} all-to-all(bf16[32,24,128]{2,1,0:T(8,128)(2,1)S(1)} %multiply.3), channel_id=1, replica_groups=mesh['xl'=2,'y'=8,'c'=2,'xh'=2,'z'=8] {'xl','xh','z'}, dimensions={0} | all-to-all | bytes 393216 | tf_op jit(solution)/shard_map/cond/branch_0_fun/all_to_all | solution.py:345
  48.8 0.3 finish.3
  49.2 0.0 copy-start.3
  49.2 0.6 %copy-done.3 = bf16[64,256]{1,0:T(8,128)(2,1)} copy-done((bf16[64,256]{1,0:T(8,128)(2,1)}, bf16[64,256]{1,0:T(8,128)(2,1)S(1)}, u32[]{:S(2)}) %copy-start.3) | copy-done | bytes 32792
  (1 shorter events, 0.0 us)
Async XLA Ops:
  2.1 18.9 %all-to-all-start.3 = ((bf16[16,16,512]{2,1,0:T(8,128)(2,1)}), bf16[16,16,512]{2,1,0:T(8,128)(2,1)S(1)}, u32[]{:S(2)}, u32[]{:S(2)}) async-start(bf16[16,16,512]{2,1,0:T(8,128)(2,1)} %get-tuple-element.99), calls=%async_computation.3 | async-start | bytes 524288 | tf_op jit(solution)/shard_map/all_to_all | solution.py:304
  11.3 4.2 %copy-start = (s32[1024]{0:T(1024)S(1)}, s32[1024]{0:T(1024)}, u32[]{:S(2)}) copy-start(s32[1024]{0:T(1024)} %virt_ref.1) | copy-start | bytes 12292
  11.3 4.4 %copy-start.1 = (s32[64]{0:T(128)S(1)}, s32[64]{0:T(128)}, u32[]{:S(2)}) copy-start(s32[64]{0:T(128)} %occ_ref.1) | copy-start | bytes 772
  11.3 4.4 %copy-start.2 = (s32[8]{0:T(128)S(1)}, s32[8]{0:T(128)}, u32[]{:S(2)}) copy-start(s32[8]{0:T(128)} %slab_ref.1) | copy-start | bytes 100
  12.0 11.2 %collective-permute-start = (bf16[256,512]{1,0:T(8,128)(2,1)S(1)}, bf16[256,512]{1,0:T(8,128)(2,1)S(1)}, u32[]{:S(2)}, u32[]{:S(2)}) collective-permute-start(bf16[256,512]{1,0:T(8,128)(2,1)S(1)} %squeeze_amp.1), channel_id=1, source_target_pairs={{0,256},{256,0},{1,257},{257,1},{2,258},{258,2},{3,259},{259,3},{4... | collective-permute-start | bytes 786440 | tf_op jit(solution)/shard_map/ppermute | solution.py:315
  49.2 0.6 %copy-start.3 = (bf16[64,256]{1,0:T(8,128)(2,1)}, bf16[64,256]{1,0:T(8,128)(2,1)S(1)}, u32[]{:S(2)}) copy-start(bf16[64,256]{1,0:T(8,128)(2,1)S(1)} %get-tuple-element.124) | copy-start | bytes 98308

commit v6 on v5

--- a/solution.py
+++ b/solution.py
@@ -210,25 +210,37 @@
     return total
 
 
-def multiply_kernel(span, move_ref, tag_ref, columns_ref, rows_ref, amp_ref, partner_ref, out_ref, sorted_ref):
+def masked_sums(rows, columns_of, tags, columns):
+    sums = lax.dot_general(rows, columns_of, (((1,), (1,)), ((), ())), preferred_element_type=F32)
+    return jnp.where(jnp.concatenate([tags] * (sums.shape[1] // LANES), 1) == columns, sums, 0.0)
+
+
+def multiply_own_kernel(move_ref, tag_ref, columns_ref, rows_ref, amp_ref, sorted_ref, sums_ref):
     cores, windows = rows_ref.shape[:2]
     per = LANES // RUN
-    halves = amp_ref.shape[0] // LANES
-    share = lax.axis_index("xl")
     for r in range(windows // per):
-        block = jnp.concatenate([x for w in range(r * per, (r + 1) * per) for x in [rows_ref[core, w] for core in range(cores)]], 0)
+        block = jnp.concatenate([rows_ref[core, w] for w in range(r * per, (r + 1) * per) for core in range(cores)], 0)
         sorted_ref[r * LANES : (r + 1) * LANES, :] = jnp.dot(
             move_ref[r], block, preferred_element_type=F32
         ).astype(BF16)
-    for side, columns_of in enumerate((amp_ref, partner_ref)):
+    for r in range(windows // per):
+        at = slice(r * LANES, (r + 1) * LANES)
+        sums_ref[at, :] = masked_sums(sorted_ref[at, :], amp_ref[...], tag_ref[at, :], columns_ref[0:1, :])
+
+
+def multiply_kernel(span, tag_ref, columns_ref, sorted_ref, own_ref, partner_ref, out_ref):
+    windows = sorted_ref.shape[0] // RUN
+    per = LANES // RUN
+    halves = partner_ref.shape[0] // LANES
+    share = lax.axis_index("xl")
+    for side in range(2):
         first = (share if side == 0 else 1 - share) * windows
         for r in range(windows // per):
             at = slice(r * LANES, (r + 1) * LANES)
-            sums = lax.dot_general(
-                sorted_ref[at, :], columns_of[...], (((1,), (1,)), ((), ())), preferred_element_type=F32
-            )
-            tags = jnp.concatenate([tag_ref[at, :]] * halves, 1)
-            sums = jnp.where(tags == columns_ref[8 * side : 8 * side + 1, :], sums, 0.0)
+            if side == 0:
+                sums = own_ref[at, :]
+            else:
+                sums = masked_sums(sorted_ref[at, :], partner_ref[...], tag_ref[at, :], columns_ref[8:9, :])
             for w in range(per):
                 total = folded(sums[w * RUN : (w + 1) * RUN], span)
                 largest = jnp.max(jnp.max(jnp.abs(total), axis=0, keepdims=True), axis=1, keepdims=True)
@@ -332,16 +344,15 @@
         name="plan",
     )(irrep_virt, irrep_occ, irrep_slab, labels)
 
-    def rest(span, move, tags, column_labels, place, row_labels, both, amp_small, amp_partner):
+    def rest(span, tags, column_labels, place, row_labels, rows, own_sums, amp_partner):
         parts = pl.pallas_call(
             functools.partial(multiply_kernel, span),
             out_shape=shaped((2 * chips, columns // LANES * span, LANES), BF16),
-            in_specs=[VMEM] * 6,
+            in_specs=[VMEM] * 5,
             out_specs=VMEM,
-            scratch_shapes=[pltpu.VMEM((chips * RUN, depth), BF16)],
             compiler_params=params(),
             name="multiply",
-        )(move, tags, column_labels, both, amp_small, amp_partner)
+        )(tags, column_labels, rows, own_sums, amp_partner)
         parts = lax.all_to_all(parts, ("xl", "xh", "z"), 0, 0, tiled=False)
         return pl.pallas_call(
             functools.partial(finish_kernel, span),
@@ -355,11 +366,21 @@
     tier = sum((most[0] >= span).astype(I32) for span in SPANS)
     own, amp_small, tier, *plan = lax.optimization_barrier((own, amp_small, tier, *plan))
     both = lax.all_gather(own, "c", axis=0, tiled=False)
+    move, tags, column_labels, place, row_labels = plan
+    rows, own_sums = pl.pallas_call(
+        multiply_own_kernel,
+        out_shape=(shaped((chips * RUN, depth), BF16), shaped((chips * RUN, columns), F32)),
+        in_specs=[VMEM] * 5,
+        out_specs=(VMEM, VMEM),
+        compiler_params=params(),
+        cost_estimate=pl.CostEstimate(flops=2 << 30, transcendentals=0, bytes_accessed=4 << 20),
+        name="multiply_own",
+    )(move, tags, column_labels, both, amp_small)
 
     return lax.switch(
         tier,
         [functools.partial(rest, span) for span in (*SPANS, RUN + 8)],
-        *plan, both, amp_small, amp_partner,
+        tags, column_labels, place, row_labels, rows, own_sums, amp_partner,
     )
 
 

time: 50.1 us -> 50.3 us (level)
    pallas_call x0 -> x1, Pallas kernels: none -> 0.61 us  [per_device(): pl.pallas_call(multiply_own_kernel, out_shape=(shaped((chips * RUN, depth...]
  transfers between devices with their start and end apart: 2 -> 2, of which waited for: 1 -> 1; matrix products, arithmetic and copies ran while one was open for 0% -> 0% of each run, Pallas kernels for 4% -> 6%
where the time goes in v6:
time: 50.3 us; the launch traced here: 50 us
  blocking collectives  26.5 us (53%)
  starting transfers between devices  12.6 us (25%)
  Pallas kernels  6.02 us (12%)
  waiting for transfers between devices  2.57 us (5%)
  between operations  1.41 us (3%)
  local copies, waits for them, and re-layouts  0.84 us (2%)
    all_to_all x1, blocking collectives, rest(): parts = lax.all_to_all(parts, ('xl', 'xh', 'z'), 0, 0, tiled=False)  24.4 us
    all_to_all x1, starting transfers between devices, per_device(): own = lax.all_to_all(small, ('xl', 'y'), 0, 0, tiled=False)  9.16 us
    ppermute x1, starting transfers between devices, per_device(): amp_partner = lax.ppermute(amp_small, 'xl', [(0, 1), (1, 0)])  3.42 us
    all_to_all x1, waiting for transfers between devices, per_device(): own = lax.all_to_all(small, ('xl', 'y'), 0, 0, tiled=False)  2.57 us
    all_gather x1, blocking collectives, per_device(): both = lax.all_gather(own, 'c', axis=0, tiled=False)  2.17 us
    pallas_call x1, Pallas kernels, per_device(): pl.pallas_call(functools.partial(squeeze_int_kernel, va_axes, vb_axes), o...  2.09 us
    pallas_call x1, Pallas kernels, per_device(): pl.pallas_call(functools.partial(plan_kernel, a_rows, va_axes, vb_axes),...  1.45 us
  transfers between devices with their start and end apart: 2, of which 1 were waited for; matrix products, arithmetic and copies ran while one was open for 0% of the time, Pallas kernels for 6%

profile of v6, /device:TPU:8, one launch (start us, length us, event | category | flops | bytes accessed | tf_op | source)
XLA Modules:
  0.0 50.0 jit_solution(13596848722401074584)
XLA Ops:
  0.0 2.1 %squeeze_int.1 = (bf16[16,16,512]{2,1,0:T(8,128)(2,1)}, bf16[256,4096]{1,0:T(8,128)(2,1)S(1)}, s32[32,128]{1,0:T(8,128)S(1)}, s32[256,128]{1,0:T(8,128)S(1)}) custom-call(s32[1024]{0:T(1024)} %virt_ref.1, s32[64]{0:T(128)} %occ_ref.1, s32[8]{0:T(128)} %slab_ref.1, bf16[32,4096]{1,0:T(8,128)(2,1)} %int_hbm.1, bf16[256,4096]{1,0:T(8,128)(2,1)} %bitcast.5), custom_call_target="tpu_custom_call" | custom-call | tf_op jit(solution)/shard_map/squeeze_int/pallas_call | solution.py:295
  2.1 9.2 %all-to-all-start.3 = ((bf16[16,16,512]{2,1,0:T(8,128)(2,1)}), bf16[16,16,512]{2,1,0:T(8,128)(2,1)S(1)}, u32[]{:S(2)}, u32[]{:S(2)}) async-start(bf16[16,16,512]{2,1,0:T(8,128)(2,1)} %get-tuple-element.92), calls=%async_computation.3 | async-start | bytes 524288 | tf_op jit(solution)/shard_map/all_to_all | solution.py:316
  11.3 0.0 copy-start
  11.3 0.0 copy-start.1
  11.3 0.0 copy-start.2
  11.3 0.7 %squeeze_amp.1.amp_ref = bf16[256,512]{1,0:T(8,128)(2,1)S(1)} custom-call(s32[32,128]{1,0:T(8,128)S(1)} %get-tuple-element.93.pair_ref, s32[256,128]{1,0:T(8,128)S(1)} %get-tuple-element.94.left_ref, bf16[256,4096]{1,0:T(8,128)(2,1)S(1)} %get-tuple-element.95.amp_ref), custom_call_target="tpu_custom_call" | custom-call | flops 4294967296 | bytes 8388608 | tf_op jit(solution)/shard_map/squeeze_amp/pallas_call | solution.py:318
  12.0 3.4 %collective-permute-start = (bf16[256,512]{1,0:T(8,128)(2,1)S(1)}, bf16[256,512]{1,0:T(8,128)(2,1)S(1)}, u32[]{:S(2)}, u32[]{:S(2)}) collective-permute-start(bf16[256,512]{1,0:T(8,128)(2,1)S(1)} %squeeze_amp.1.amp_ref), channel_id=1, source_target_pairs={{0,256},{256,0},{1,257},{257,1},{2,258},{258,2},{3,259},{259,3},{4... | collective-permute-start | bytes 786440 | tf_op jit(solution)/shard_map/ppermute | solution.py:327
  15.5 0.0 copy-done
  15.5 0.1 reshape.17
  15.6 0.1 reshape.18.labels_ref
  15.7 0.0 copy-done.1
  15.7 0.0 copy-done.2
  15.7 1.4 %plan.1 = (bf16[4,128,128]{2,1,0:T(8,128)(2,1)S(1)}, s32[512,128]{1,0:T(8,128)S(1)}, s32[16,256]{1,0:T(8,128)S(1)}, s32[64,128]{1,0:T(8,128)S(1)}, s32[64,256]{1,0:T(8,128)S(1)}, /*index=5*/s32[1]{0:T(128)}) custom-call(s32[1024]{0:T(1024)S(1)} %copy-done, s32[64]{0:T(128)S(1)} %copy-done.1, s32[8]{0:T(128)S(1)} %copy-done.2, s32[8,128]{1,0:T(8,128)S(1)} %reshape.18.labels_ref), custom_call_target="tpu_custom_call" | custom-call | flops 2147483648 | bytes 4194304 | tf_op jit(solution)/shard_map/plan/pallas_call | solution.py:330
  18.5 2.6 %all-to-all-done.3 = bf16[16,16,512]{2,1,0:T(8,128)(2,1)S(1)} async-done(((bf16[16,16,512]{2,1,0:T(8,128)(2,1)}), bf16[16,16,512]{2,1,0:T(8,128)(2,1)S(1)}, u32[]{:S(2)}, u32[]{:S(2)}) %all-to-all-start.3) | async-done | bytes 262176 | tf_op jit(solution)/shard_map/all_to_all | solution.py:316
  21.0 2.2 %all-gather = bf16[32,16,512]{2,1,0:T(8,128)(2,1)S(1)} all-gather(bf16[16,16,512]{2,1,0:T(8,128)(2,1)S(1)} %all-to-all-done.3), channel_id=2, replica_groups=mesh['xl'=2,'y'=8,'c'=2,'xh'=2,'z'=8] {'c'}, dimensions={0}, use_global_device_ids=true | all-gather | bytes 786432 | tf_op jit(solution)/shard_map/all_gather | solution.py:368
  23.2 0.6 %multiply_own.1 = (bf16[512,512]{1,0:T(8,128)(2,1)S(1)}, f32[512,256]{1,0:T(8,128)S(1)}) custom-call(bf16[4,128,128]{2,1,0:T(8,128)(2,1)S(1)} %get-tuple-element.105.move_ref, s32[512,128]{1,0:T(8,128)S(1)} %get-tuple-element.103.tag_ref, s32[16,256]{1,0:T(8,128)S(1)} %get-tuple-element.104.columns_ref, bf16[2,16,16,512]{3,2,1,0:T(8,128)(2,1)S(1)} %bitcast.4, ...), custom_call_target="tpu_custom_call" | custom-call | flops 2147483648 | bytes 4194304 | tf_op jit(solution)/shard_map/multiply_own/pallas_call | solution.py:370
  23.8 0.0 collective-permute-done
  23.8 25.5 %conditional.1 = (bf16[64,256]{1,0:T(8,128)(2,1)S(1)}) conditional(s32[]{:T(128)} %clamp.3, (s32[512,128]{1,0:T(8,128)S(1)}, s32[16,256]{1,0:T(8,128)S(1)}, bf16[512,512]{1,0:T(8,128)(2,1)S(1)}, f32[512,256]{1,0:T(8,128)S(1)}, bf16[256,512]{1,0:T(8,128)(2,1)S(1)}, /*index=5*/s32[64,128]{1,0:T(8,128)S(1)}, ...), branch_computations={%region_0.0_spmd, %region_1.0_spmd, %region_2.0_spmd} | conditional | bytes 1310728 | solution.py:380
  23.8 0.8 %multiply.3 = bf16[32,24,128]{2,1,0:T(8,128)(2,1)S(1)} custom-call(s32[512,128]{1,0:T(8,128)S(1)} %get-tuple-element.54.tag_ref, s32[16,256]{1,0:T(8,128)S(1)} %get-tuple-element.50.columns_ref, bf16[512,512]{1,0:T(8,128)(2,1)S(1)} %get-tuple-element.55.sorted_ref, f32[512,256]{1,0:T(8,128)S(1)} %get-tuple-element.56.own_ref, ...), custom_call_target="tpu_custom_call" | custom-call | tf_op jit(solution)/shard_map/cond/branch_0_fun/multiply/pallas_call | solution.py:348
  24.7 24.4 %all_to_all.17.parts_ref = bf16[32,24,128]{2,1,0:T(8,128)(2,1)S(1)} all-to-all(bf16[32,24,128]{2,1,0:T(8,128)(2,1)S(1)} %multiply.3), channel_id=1, replica_groups=mesh['xl'=2,'y'=8,'c'=2,'xh'=2,'z'=8] {'xl','xh','z'}, dimensions={0} | all-to-all | bytes 393216 | tf_op jit(solution)/shard_map/cond/branch_0_fun/all_to_all | solution.py:356
  49.0 0.3 finish.3
  49.4 0.0 copy-start.3
  49.4 0.6 %copy-done.3 = bf16[64,256]{1,0:T(8,128)(2,1)} copy-done((bf16[64,256]{1,0:T(8,128)(2,1)}, bf16[64,256]{1,0:T(8,128)(2,1)S(1)}, u32[]{:S(2)}) %copy-start.3) | copy-done | bytes 32792
  (1 shorter events, 0.0 us)
Async XLA Ops:
  2.1 18.9 %all-to-all-start.3 = ((bf16[16,16,512]{2,1,0:T(8,128)(2,1)}), bf16[16,16,512]{2,1,0:T(8,128)(2,1)S(1)}, u32[]{:S(2)}, u32[]{:S(2)}) async-start(bf16[16,16,512]{2,1,0:T(8,128)(2,1)} %get-tuple-element.92), calls=%async_computation.3 | async-start | bytes 524288 | tf_op jit(solution)/shard_map/all_to_all | solution.py:316
  11.3 4.2 %copy-start = (s32[1024]{0:T(1024)S(1)}, s32[1024]{0:T(1024)}, u32[]{:S(2)}) copy-start(s32[1024]{0:T(1024)} %virt_ref.1) | copy-start | bytes 12292
  11.3 4.4 %copy-start.1 = (s32[64]{0:T(128)S(1)}, s32[64]{0:T(128)}, u32[]{:S(2)}) copy-start(s32[64]{0:T(128)} %occ_ref.1) | copy-start | bytes 772
  11.3 4.4 %copy-start.2 = (s32[8]{0:T(128)S(1)}, s32[8]{0:T(128)}, u32[]{:S(2)}) copy-start(s32[8]{0:T(128)} %slab_ref.1) | copy-start | bytes 100
  12.0 11.8 %collective-permute-start = (bf16[256,512]{1,0:T(8,128)(2,1)S(1)}, bf16[256,512]{1,0:T(8,128)(2,1)S(1)}, u32[]{:S(2)}, u32[]{:S(2)}) collective-permute-start(bf16[256,512]{1,0:T(8,128)(2,1)S(1)} %squeeze_amp.1.amp_ref), channel_id=1, source_target_pairs={{0,256},{256,0},{1,257},{257,1},{2,258},{258,2},{3,259},{259,3},{4... | collective-permute-start | bytes 786440 | tf_op jit(solution)/shard_map/ppermute | solution.py:327
  49.4 0.6 %copy-start.3 = (bf16[64,256]{1,0:T(8,128)(2,1)}, bf16[64,256]{1,0:T(8,128)(2,1)S(1)}, u32[]{:S(2)}) copy-start(bf16[64,256]{1,0:T(8,128)(2,1)S(1)} %get-tuple-element.119) | copy-start | bytes 98308
